TPU v7x, 32 devices: a whole 2x2x4 slice. The times are simulated.
32 devices in a mesh: nodes: 16 (over z, y, core), hid: 2 (over x).
Axes of the slice: x: 2, y: 2, z: 4, core: 2. Of those that a mesh axis runs over, the one named last changes fastest.
Arguments:
- features: bfloat16 [24576, 512], P(('nodes', 'hid')), may hold values from -6 to 6
- levels: int32 [24576], P(('nodes', 'hid')), may hold values from 0 to 1
- neighbour_index: int32 [24576, 16], P(('nodes', 'hid')), may hold values from 0 to 24575, as said below
- neighbour_count: int32 [24576], P(('nodes', 'hid')), may hold values from 2 to 16
- cotangent: bfloat16 [24576, 512], P(('nodes', 'hid')), may hold values from -6 to 6
- attention_weight: float32 [4, 512, 512], replicated
- up_weight: float32 [512, 2048], P(None, 'hid'), may hold values from -0.25 to 0.25
- down_weight: float32 [2048, 512], P('hid'), may hold values from -0.125 to 0.125
- modulation: float32 [2, 4, 512], replicated, may hold values from -0.5 to 0.5
- attention_moment: float32 [4, 512, 512], P(None, 'hid')
- up_moment: float32 [512, 2048], P(None, 'hid')
- down_moment: float32 [2048, 512], P('hid')
- modulation_moment: float32 [2, 4, 512], P(None, 'hid')
Outputs:
- output: bfloat16 [24576, 512], P(('nodes', 'hid'))
- features_grad: float32 [24576, 512], P(('nodes', 'hid'))
- attention_moment_new: float32 [4, 512, 512], P(None, 'hid')
- attention_new: float32 [4, 512, 512], P(None, 'hid')
- up_moment_new: float32 [512, 2048], P(None, 'hid')
- up_new: float32 [512, 2048], P(None, 'hid')
- down_moment_new: float32 [2048, 512], P('hid')
- down_new: float32 [2048, 512], P('hid')
- modulation_moment_new: float32 [2, 4, 512], P(None, 'hid')
- modulation_new: float32 [2, 4, 512], P(None, 'hid')
Inputs may be any that keep to these rules, and one draw needn't show every extreme that they name: `neighbour_index`: slot 0 of every node names the node itself; every slot names a node whose index is at most 192 from the node's own, and slot 1 names the node exactly 192 away wherever that index exists. Slots past a node's count also hold valid indices.
All inputs are finite; a program needn't handle non-finite values.
Results may differ from a plain program's by a relative error of at most 0.018.
The roundings to bfloat16 on the way count: a program that leaves them out, or rounds other values in their place, can miss the bound.
Values may be sent and summed in bfloat16 or wider, within the bound.
No kernel may reach another device: no remote copies, remote signals or barrier semaphores. Data moves between devices by JAX's collectives and lax.ppermute only.
A program may use at most 192 MiB of HBM per device.

v0:
```python
import math

import jax
import jax.numpy as jnp
from jax import lax
from jax.sharding import PartitionSpec as P

D = 512
HEADS = 4
HD = 128
FF = 2048
K = 16
LEVELS = 2
NS_STEPS = 4


highest = lax.Precision.HIGHEST
ns_first = 3.4445
ns_second = -4.775
ns_third = 2.0315
momentum_rate = 0.95
vector_rate = 0.9
muon_rate = 0.2
decay_rate = 0.1


def passed_along(block, axis, distance):
    devices = range(lax.axis_size(axis))
    route = [(i - distance, i) for i in devices if i - distance in devices]
    return lax.ppermute(block, axis, route)


def padded_2(cells, sides, width):
    for axis, dim in sides:
        count = lax.axis_size(axis)
        ends = count - 1
        head = lax.slice_in_dim(cells, 0, width, axis=dim)
        tail = lax.slice_in_dim(cells, cells.shape[dim] - width, cells.shape[dim], axis=dim)
        cells = jnp.concatenate(
            [
                lax.ppermute(tail, axis, [(i, (i + 1) % count) for i in range(ends)]),
                cells,
                lax.ppermute(head, axis, [((i + 1) % count, i) for i in range(ends)]),
            ],
            axis=dim,
        )
    return cells


def block_length(row_count):
    for length in range(min(row_count, 1024), 0, -1):
        if row_count % length == 0:
            return length
    return row_count


def modulate_rows(field, picked, modulation, column):
    average = jnp.mean(field, axis=-1, keepdims=True)
    centred = field - average
    variance = jnp.mean(centred * centred, axis=-1, keepdims=True)
    inverse = lax.rsqrt(variance + 1e-06)
    normed = centred * inverse
    scale_rows = jnp.dot(
        picked, modulation[:, column, :], precision=highest, preferred_element_type=jnp.float32
    )
    shift_rows = jnp.dot(
        picked, modulation[:, column + 1, :], precision=highest, preferred_element_type=jnp.float32
    )
    return (normed * (1.0 + scale_rows) + shift_rows, normed, inverse, scale_rows)


def norm_back(grad_out, normed, inverse, scale_rows, picked):
    grad_norm = grad_out * (1.0 + scale_rows)
    grad_in = inverse * (
        grad_norm
        - jnp.mean(grad_norm, axis=-1, keepdims=True)
        - normed * jnp.mean(grad_norm * normed, axis=-1, keepdims=True)
    )
    grad_scale = jnp.einsum("rl,rd->ld", picked, grad_out * normed, precision=highest)
    grad_shift = jnp.einsum("rl,rd->ld", picked, grad_out, precision=highest)
    return (grad_in, grad_scale, grad_shift)


def split_parts(dense):
    upper = dense.astype(jnp.bfloat16)
    lower = (dense - upper.astype(jnp.float32)).astype(jnp.bfloat16)
    return (upper, lower)


def dense_times(dense, window_rows):
    upper, lower = split_parts(dense)
    first = jnp.einsum("bhw,whd->bhd", upper, window_rows, preferred_element_type=jnp.float32)
    return first + jnp.einsum(
        "bhw,whd->bhd", lower, window_rows, preferred_element_type=jnp.float32
    )


def dense_back(dense, row_values):
    upper, lower = split_parts(dense)
    first = jnp.einsum("bhw,bhd->whd", upper, row_values, preferred_element_type=jnp.float32)
    return first + jnp.einsum("bhw,bhd->whd", lower, row_values, preferred_element_type=jnp.float32)


def attend(queries, local_index, live_count, start, padded, span):
    row_count = queries.shape[0]
    window = lax.dynamic_slice_in_dim(padded, start, span, 1)
    window_keys = window[0].reshape(span, HEADS, HD)
    window_values = window[1].reshape(span, HEADS, HD)
    positions = (local_index - start).astype(jnp.int32)
    chooser = (positions[:, :, None] == jnp.arange(span, dtype=jnp.int32)[None, None, :]).astype(
        jnp.float32
    )
    heads_query = queries.reshape(row_count, HEADS, HD)
    full_scores = jnp.einsum(
        "bhd,whd->bhw", heads_query, window_keys, preferred_element_type=jnp.float32
    )
    scores = jnp.einsum("bkw,bhw->bhk", chooser, full_scores, precision=highest) * (
        1.0 / math.sqrt(HD)
    )
    live_slots = (jnp.arange(K, dtype=jnp.int32)[None, :] < live_count[:, None])[:, None, :]
    return (scores, live_slots, heads_query, chooser, window_keys, window_values)


def forward_block(inputs, padded, span):
    queries, local_index, live_count, start = inputs
    row_count = queries.shape[0]
    scores, live_slots, heads_query, chooser, window_keys, window_values = attend(
        queries, local_index, live_count, start, padded, span
    )
    masked = jnp.where(live_slots, scores, -1e30)
    peak_score = jnp.max(masked, axis=-1, keepdims=True)
    exponent = jnp.where(live_slots, jnp.exp(masked - peak_score), 0.0)
    totals = jnp.sum(exponent, axis=-1, keepdims=True)
    weights = (exponent / totals).astype(jnp.bfloat16)
    spread_weights = jnp.einsum(
        "bkw,bhk->bhw", chooser, weights.astype(jnp.float32), precision=highest
    )
    attended = dense_times(spread_weights, window_values)
    return (
        attended.reshape(row_count, HEADS * HD).astype(jnp.bfloat16),
        (peak_score + jnp.log(totals))[..., 0],
    )


def backward_block(buffer, inputs, padded, span):
    queries, local_index, live_count, start, log_totals, grad_attended = inputs
    row_count = queries.shape[0]
    scores, live_slots, heads_query, chooser, window_keys, window_values = attend(
        queries, local_index, live_count, start, padded, span
    )
    probs = jnp.where(live_slots, jnp.exp(scores - log_totals[..., None]), 0.0)
    weights = probs.astype(jnp.bfloat16)
    grad_heads = grad_attended.reshape(row_count, HEADS, HD)
    full_grads = jnp.einsum(
        "bhd,whd->bhw", grad_heads, window_values, preferred_element_type=jnp.float32
    )
    grad_probs = jnp.einsum("bkw,bhw->bhk", chooser, full_grads, precision=highest)
    grad_scores = (
        probs * (grad_probs - jnp.sum(probs * grad_probs, axis=-1, keepdims=True))
    ).astype(jnp.bfloat16)
    factor = 1.0 / math.sqrt(HD)
    spread_scores = jnp.einsum(
        "bkw,bhk->bhw", chooser, grad_scores.astype(jnp.float32), precision=highest
    )
    spread_weights = jnp.einsum(
        "bkw,bhk->bhw", chooser, weights.astype(jnp.float32), precision=highest
    )
    grad_query = dense_times(spread_scores, window_keys) * factor
    grad_key = dense_back(spread_scores, heads_query) * factor
    grad_value = dense_back(spread_weights, grad_heads)
    stacked = jnp.stack([grad_key, grad_value]).reshape(2, span, HEADS * HD)
    current = lax.dynamic_slice_in_dim(buffer, start, span, 1)
    buffer = lax.dynamic_update_slice_in_dim(buffer, current + stacked, start, 1)
    return (buffer, grad_query.reshape(row_count, HEADS * HD))


def pass_rim(piece, offset):
    return passed_along(piece.astype(jnp.bfloat16), ("nodes", "hid"), offset).astype(piece.dtype)


def schulz_update(current_attn, current_up, current_down, gram_attn, gram_up, gram_down):
    poly_attn = (
        ns_second * gram_attn.astype(jnp.float32)
        + ns_third
        * jnp.einsum("pcd,pde->pce", gram_attn, gram_attn, preferred_element_type=jnp.float32)
    ).astype(jnp.bfloat16)
    poly_up = (
        ns_second * gram_up.astype(jnp.float32)
        + ns_third * jnp.dot(gram_up, gram_up, preferred_element_type=jnp.float32)
    ).astype(jnp.bfloat16)
    poly_down = (
        ns_second * gram_down.astype(jnp.float32)
        + ns_third * jnp.dot(gram_down, gram_down, preferred_element_type=jnp.float32)
    ).astype(jnp.bfloat16)
    next_attn = (
        ns_first * current_attn.astype(jnp.float32)
        + jnp.einsum("prc,pcd->prd", current_attn, poly_attn, preferred_element_type=jnp.float32)
    ).astype(jnp.bfloat16)
    next_up = (
        ns_first * current_up.astype(jnp.float32)
        + jnp.dot(poly_up, current_up, preferred_element_type=jnp.float32)
    ).astype(jnp.bfloat16)
    next_down = (
        ns_first * current_down.astype(jnp.float32)
        + jnp.dot(current_down, poly_down, preferred_element_type=jnp.float32)
    ).astype(jnp.bfloat16)
    return (next_attn, next_up, next_down)


def on_device(
    features,
    levels,
    neighbour_index,
    neighbour_count,
    cotangent,
    attention_weight,
    up_weight,
    down_weight,
    modulation,
    attention_moment,
    up_moment,
    down_moment,
    modulation_moment,
):
    row_count, model_width = features.shape
    rim_rows = row_count // 4
    first_row = lax.axis_index(("nodes", "hid")) * row_count
    picked = (levels[:, None] == jnp.arange(LEVELS, dtype=jnp.int32)[None, :]).astype(jnp.float32)
    stream = features.astype(jnp.float32)
    attn_bf = attention_weight.astype(jnp.bfloat16)
    first_in, normed_one, inverse_one, scale_one = modulate_rows(stream, picked, modulation, 0)
    first_in = first_in.astype(jnp.bfloat16)
    projected = jnp.einsum(
        "rd,pde->pre", first_in, attn_bf[:3], preferred_element_type=jnp.float32
    ).astype(jnp.bfloat16)
    padded = padded_2(projected[1:], ((("nodes", "hid"), 1),), rim_rows)
    local_index = neighbour_index - first_row + rim_rows
    block_rows = block_length(row_count)
    block_count = row_count // block_rows
    span = block_rows + 2 * rim_rows
    starts = (jnp.arange(block_count, dtype=jnp.int32) * block_rows).astype(jnp.int32)
    blocked = (
        projected[0].reshape(block_count, block_rows, model_width),
        local_index.reshape(block_count, block_rows, K),
        neighbour_count.reshape(block_count, block_rows),
        starts,
    )
    attended, log_totals = lax.map(lambda inputs: forward_block(inputs, padded, span), blocked)
    attended = attended.reshape(row_count, model_width)
    hidden_state = stream + jnp.dot(attended, attn_bf[3], preferred_element_type=jnp.float32)
    second_in, normed_two, inverse_two, scale_two = modulate_rows(
        hidden_state, picked, modulation, 2
    )
    second_in = second_in.astype(jnp.bfloat16)
    up_bf = up_weight.astype(jnp.bfloat16)
    down_bf = down_weight.astype(jnp.bfloat16)
    inputs_all = lax.all_gather(second_in, "hid", axis=0, tiled=True)
    preact = jnp.dot(inputs_all, up_bf, preferred_element_type=jnp.float32)
    activation = jax.nn.silu(preact).astype(jnp.bfloat16)
    branch = lax.psum_scatter(
        jnp.dot(activation, down_bf, preferred_element_type=jnp.float32).astype(jnp.bfloat16),
        "hid",
        scatter_dimension=0,
        tiled=True,
    ).astype(jnp.float32)
    output = (hidden_state + branch).astype(jnp.bfloat16)
    grad_out = cotangent.astype(jnp.float32)
    sigmoid_pre = jax.nn.sigmoid(preact)
    slope_pre = sigmoid_pre * (1.0 + preact * (1.0 - sigmoid_pre))
    cot_all = lax.all_gather(cotangent, "hid", axis=0, tiled=True)
    grad_act = jnp.einsum("rd,fd->rf", cot_all, down_bf, preferred_element_type=jnp.float32)
    grad_down = jnp.einsum("rf,rd->fd", activation, cot_all, preferred_element_type=jnp.float32)
    grad_pre = (grad_act * slope_pre).astype(jnp.bfloat16)
    grad_up = jnp.einsum("rd,rf->df", inputs_all, grad_pre, preferred_element_type=jnp.float32)
    grad_second = lax.psum_scatter(
        jnp.einsum("rf,df->rd", grad_pre, up_bf, preferred_element_type=jnp.float32).astype(
            jnp.bfloat16
        ),
        "hid",
        scatter_dimension=0,
        tiled=True,
    ).astype(jnp.float32)
    grad_hidden, grad_scale_two, grad_shift_two = norm_back(
        grad_second, normed_two, inverse_two, scale_two, picked
    )
    grad_hidden = grad_out + grad_hidden
    grad_branch = grad_hidden.astype(jnp.bfloat16)
    grad_attended = jnp.einsum(
        "re,de->rd", grad_branch, attn_bf[3], preferred_element_type=jnp.float32
    ).astype(jnp.bfloat16)
    grad_wout = jnp.einsum("rd,re->de", attended, grad_branch, preferred_element_type=jnp.float32)
    empty_buffer = jnp.zeros((2, row_count + 2 * rim_rows, model_width), jnp.float32)
    scan_inputs = blocked + (
        log_totals,
        grad_attended.reshape(block_count, block_rows, model_width),
    )
    kv_buffer, grad_query = lax.scan(
        lambda buffer, inputs: backward_block(buffer, inputs, padded, span),
        empty_buffer,
        scan_inputs,
    )
    from_above = pass_rim(kv_buffer[:, :rim_rows], -1)
    from_below = pass_rim(kv_buffer[:, row_count + rim_rows :], 1)
    own_grads = kv_buffer[:, rim_rows : rim_rows + row_count]
    own_grads = own_grads.at[:, :rim_rows].add(from_below)
    own_grads = own_grads.at[:, row_count - rim_rows :].add(from_above)
    grad_qkv = jnp.concatenate(
        [grad_query.reshape(1, row_count, model_width), own_grads], axis=0
    ).astype(jnp.bfloat16)
    grad_first = jnp.einsum(
        "pre,pde->rd", grad_qkv, attn_bf[:3], preferred_element_type=jnp.float32
    )
    grad_wqkv = jnp.einsum("rd,pre->pde", first_in, grad_qkv, preferred_element_type=jnp.float32)
    grad_stream, grad_scale_one, grad_shift_one = norm_back(
        grad_first, normed_one, inverse_one, scale_one, picked
    )
    features_grad = grad_hidden + grad_stream
    grad_attn = jnp.concatenate([grad_wqkv, grad_wout[None]], axis=0)
    grad_table = jnp.stack([grad_scale_one, grad_shift_one, grad_scale_two, grad_shift_two], axis=1)
    attn_half, table_half = (
        lax.psum_scatter(
            grad_attn.astype(jnp.bfloat16), "hid", scatter_dimension=1, tiled=True
        ).astype(jnp.float32),
        lax.psum_scatter(
            grad_table.astype(jnp.bfloat16), "hid", scatter_dimension=1, tiled=True
        ).astype(jnp.float32),
    )
    up_half, down_half = (grad_up, grad_down)
    attn_grad, table_grad, up_grad, down_grad = lax.psum(
        (attn_half, table_half, up_half, down_half), "nodes"
    )
    hid_index = lax.axis_index("hid")
    half_rows = attn_grad.shape[1]
    table_cols = table_grad.shape[1]
    attn_own = lax.dynamic_slice_in_dim(attention_weight, hid_index * half_rows, half_rows, 1)
    table_own = lax.dynamic_slice_in_dim(modulation, hid_index * table_cols, table_cols, 1)
    attention_moment_new = momentum_rate * attention_moment + attn_grad
    up_moment_new = momentum_rate * up_moment + up_grad
    down_moment_new = momentum_rate * down_moment + down_grad
    blend_attn = attn_grad + momentum_rate * attention_moment_new
    blend_up = up_grad + momentum_rate * up_moment_new
    blend_down = down_grad + momentum_rate * down_moment_new
    squares = jnp.concatenate(
        [
            jnp.sum(blend_attn * blend_attn, axis=(1, 2)),
            jnp.sum(blend_up * blend_up)[None],
            jnp.sum(blend_down * blend_down)[None],
        ]
    )
    norm_totals = lax.psum(squares, "hid")
    divisors = jnp.sqrt(norm_totals) + 1e-07
    current_attn = (blend_attn / divisors[:4, None, None]).astype(jnp.bfloat16)
    current_up = (blend_up / divisors[4]).astype(jnp.bfloat16)
    current_down = (blend_down / divisors[5]).astype(jnp.bfloat16)
    for _ in range(NS_STEPS):
        part_attn = jnp.einsum(
            "prc,prd->pcd", current_attn, current_attn, preferred_element_type=jnp.float32
        )
        part_up = jnp.einsum(
            "rc,sc->rs", current_up, current_up, preferred_element_type=jnp.float32
        )
        part_down = jnp.einsum(
            "rc,rd->cd", current_down, current_down, preferred_element_type=jnp.float32
        )
        gram_attn, gram_up, gram_down = (
            lax.psum(part_attn.astype(jnp.bfloat16), "hid").astype(jnp.float32),
            lax.psum(part_up.astype(jnp.bfloat16), "hid").astype(jnp.float32),
            lax.psum(part_down.astype(jnp.bfloat16), "hid").astype(jnp.float32),
        )
        current_attn, current_up, current_down = schulz_update(
            current_attn,
            current_up,
            current_down,
            gram_attn.astype(jnp.bfloat16),
            gram_up.astype(jnp.bfloat16),
            gram_down.astype(jnp.bfloat16),
        )
    attention_new = attn_own - muon_rate * (
        0.2 * math.sqrt(D) * current_attn.astype(jnp.float32) + decay_rate * attn_own
    )
    up_new = up_weight - muon_rate * (
        0.2 * math.sqrt(max(D, FF)) * current_up.astype(jnp.float32) + decay_rate * up_weight
    )
    down_new = down_weight - muon_rate * (
        0.2 * math.sqrt(max(D, FF)) * current_down.astype(jnp.float32) + decay_rate * down_weight
    )
    node_total = row_count * lax.axis_size(("nodes", "hid"))
    modulation_moment_new = vector_rate * modulation_moment + table_grad
    modulation_new = table_own - 0.2 / math.sqrt(node_total) * modulation_moment_new
    return (
        output,
        features_grad,
        attention_moment_new,
        attention_new,
        up_moment_new,
        up_new,
        down_moment_new,
        down_new,
        modulation_moment_new,
        modulation_new,
    )


def solution(mesh):
    placed = (
        P(("nodes", "hid"), None),
        P(("nodes", "hid")),
        P(("nodes", "hid"), None),
        P(("nodes", "hid")),
        P(("nodes", "hid"), None),
        P(),
        P(None, "hid"),
        P("hid", None),
        P(),
        P(None, "hid", None),
        P(None, "hid"),
        P("hid", None),
        P(None, "hid", None),
    )
    return jax.shard_map(
        on_device,
        mesh=mesh,
        in_specs=placed,
        out_specs=(
            P(("nodes", "hid"), None),
            P(("nodes", "hid"), None),
            P(None, "hid", None),
            P(None, "hid", None),
            P(None, "hid"),
            P(None, "hid"),
            P("hid", None),
            P("hid", None),
            P(None, "hid", None),
            P(None, "hid", None),
        ),
        check_vma=False,
    )
```

profile of v0, /device:TPU:0, one launch (start us, length us, event | category | flops | bytes accessed | tf_op | source)
XLA Modules:
  0.0 974.1 jit_solution(15321122008504157830)
XLA Ops:
  17.2 4.9 collective-permute-start
  32.0 4.1 collective-permute-done
  36.1 3.8 collective-permute-done.1
  44.5 7.1 convolution_bitcast_fusion.1
  51.6 16.5 %copy.129 = f32[768,4,1152]{2,1,0:T(4,128)} copy(f32[768,4,1152]{0,2,1:T(8,128)} %convolution_bitcast_fusion.1) | data formatting | bytes 28311552 | tf_op jit(solution)/shard_map/while/body/eval_jaxpr/bhd,whd->bhw/transpose | solution.py:114
  68.1 42.6 %select_reduce_fusion = (f32[768,4]{1,0:T(8,128)S(1)}, f32[768,4,16]{2,1,0:T(4,128)S(1)}) fusion(pred[768,16]{1,0:T(8,128)(4,1)S(1)} %copy-done.47, f32[768,4,1152]{2,1,0:T(4,128)} %copy.129, s32[768,16]{1,0:T(8,128)} %copy.128), kind=kOutput, calls=%fused_computation.132 | convolution fusion | flops 693777408 | bytes 14426112 | tf_op jit(solution)/shard_map/while/body/eval_jaxpr/bkw,bhw->bhk/dot_general | solution.py:117
  110.7 2.9 fusion.117
  113.6 16.0 %subtract_convert_fusion.2 = (bf16[768,4,1152]{2,1,0:T(4,128)(2,1)}, bf16[768,4,1152]{2,1,0:T(4,128)(2,1)}) fusion(s32[768,16]{1,0:T(8,128)S(1)} %copy-done.50, f32[768,4,16]{2,1,0:T(4,128)S(1)} %get-tuple-element.161, f32[768,4]{1,0:T(8,128)S(1)} %fusion.117, f32[768,4]{1,0:T(8,128)S(1)} %get-tuple-element.160, pred[768,16]{1,0:T(8,128)(4,1)S(1)} %copy-done.48), kind=kOutput, calls=%fused_computation.13 | convolution fusion | flops 141803520 | bytes 14438400 | tf_op jit(solution)/shard_map/while/body/eval_jaxpr/bkw,bhk->bhw/dot_general | solution.py:135
  130.8 6.0 fusion.14
  144.8 27.3 %all-gather.3.cloned.1.call-done = bf16[1536,512]{0,1:T(8,128)(2,1)} async-done(((bf16[768,512]{0,1:T(8,128)(2,1)}), bf16[1536,512]{0,1:T(8,128)(2,1)}) %all-gather.3.cloned.1.call-update) | async-done | bytes 1572880 | tf_op jit(solution)/shard_map/all_gather | solution.py:257
  172.2 8.5 multiply_convert_fusion.1
  180.7 20.3 %all-gather.5.cloned.1.call-done = bf16[1536,512]{1,0:T(8,128)(2,1)} async-done(((bf16[768,512]{1,0:T(8,128)(2,1)}), bf16[1536,512]{1,0:T(8,128)(2,1)}) %all-gather.5.cloned.1.call-update) | async-done | bytes 1572880 | tf_op jit(solution)/shard_map/all_gather | solution.py:270
  200.9 7.1 multiply_convert_fusion
  209.7 3.0 convolution_convert_fusion
  212.7 5.5 convolution_convert_fusion.1
  222.0 17.1 %subtract_convert_fusion = (bf16[768,4,1152]{2,1,0:T(4,128)(2,1)}, bf16[768,4,1152]{2,1,0:T(4,128)(2,1)}) fusion(s32[768,16]{1,0:T(8,128)} %copy.128, f32[768,4,16]{2,1,0:T(4,128)} %copy-done.36, f32[768,4]{1,0:T(8,128)S(1)} %log_add_fusion, pred[768,16]{1,0:T(8,128)(4,1)} %iota_compare_fusion.8), kind=kOutput, calls=%fused_computation.11 | convolution fusion | flops 141705216 | bytes 14426112 | tf_op jit(solution)/shard_map/while/body/eval_jaxpr/bkw,bhk->bhw/dot_general | solution.py:165
  239.2 3.1 fusion.216
  242.3 3.1 fusion.217
  247.5 20.3 %reduce-scatter.4.cloned.1.call-done = bf16[768,512]{0,1:T(8,128)(2,1)} async-done(((bf16[1536,512]{0,1:T(8,128)(2,1)}), bf16[768,512]{0,1:T(8,128)(2,1)}) %reduce-scatter.4.cloned.1.call-update) | async-done | bytes 786448 | tf_op jit(solution)/shard_map/reduce_scatter | solution.py:260
  267.8 3.6 multiply_add_fusion.6
  275.1 7.0 convolution_bitcast_fusion
  282.1 16.9 %copy.140 = f32[768,4,1152]{2,1,0:T(4,128)} copy(f32[768,4,1152]{0,2,1:T(8,128)} %convolution_bitcast_fusion) | data formatting | bytes 28311552 | tf_op jit(solution)/shard_map/while/body/eval_jaxpr/bhd,whd->bhw/transpose | solution.py:154
  299.0 43.8 %multiply_reduce_fusion.3 = (f32[768,4]{1,0:T(8,128)S(1)}, f32[768,4,16]{2,1,0:T(4,128)}) fusion(f32[768,4,16]{2,1,0:T(4,128)} %copy-done.36, f32[768,4]{1,0:T(8,128)} %copy-done.52, pred[768,16]{1,0:T(8,128)(4,1)S(1)} %copy-done.49, f32[768,4,1152]{2,1,0:T(4,128)} %copy.140, s32[768,16]{1,0:T(8,128)} %copy.128), kind=kOutput, calls=%fused_computation.113 | convolution fusion | flops 693826560 | bytes 14635008 | tf_op jit(solution)/shard_map/while/body/eval_jaxpr/bkw,bhw->bhk/dot_general | solution.py:157
  342.8 17.1 %fusion.209 = (bf16[768,4,1152]{2,1,0:T(4,128)(2,1)}, bf16[768,4,1152]{2,1,0:T(4,128)(2,1)S(1)}) fusion(s32[768,16]{1,0:T(8,128)S(1)} %copy-done.51, f32[768,4,16]{2,1,0:T(4,128)} %get-tuple-element.167, f32[768,4]{1,0:T(8,128)S(1)} %get-tuple-element.166, f32[768,4,16]{2,1,0:T(4,128)S(1)} %copy-done.37, f32[768,4]{1,0:T(8,128)S(1)} %copy-done.53, ...), kind=kOutput, calls=%fused_computation.304 | convolution fusion | flops 141803520 | bytes 14635008 | tf_op jit(solution)/shard_map/while/body/eval_jaxpr/bkw,bhk->bhw/dot_general | solution.py:162
  359.9 3.6 fusion.20
  366.3 7.6 multiply_convert_fusion.2
  373.9 2.8 fusion.33
  381.0 3.1 copy.152
  384.1 3.1 copy.151
  387.2 2.9 fusion.26
  395.2 11.2 %collective-permute-done.2 = bf16[2,192,512]{2,1,0:T(8,128)(2,1)S(1)} collective-permute-done((bf16[2,192,512]{2,1,0:T(8,128)(2,1)S(1)}, bf16[2,192,512]{2,1,0:T(8,128)(2,1)S(1)}, u32[]{:S(2)}, u32[]{:S(2)}) %collective-permute-start.2) | collective-permute-done | bytes 393248 | tf_op jit(solution)/shard_map/ppermute | solution.py:30
  406.5 4.6 collective-permute-done.3
  415.5 2.9 copy.154
  419.7 5.0 multiply_reduce_fusion.1
  433.0 5.3 all-reduce
  438.3 10.5 %reduce-scatter.8.cloned.1.call-done = bf16[4,256,512]{1,2,0:T(8,128)(2,1)} async-done(((bf16[4,512,512]{1,2,0:T(8,128)(2,1)}), bf16[4,256,512]{1,2,0:T(8,128)(2,1)}) %reduce-scatter.8.cloned.1.call-update) | async-done | bytes 1048592 | tf_op jit(solution)/shard_map/reduce_scatter | solution.py:321
  448.8 76.0 %all-reduce.23 = (f32[4,256,512]{1,2,0:T(8,128)}, f32[2,2,512]{2,0,1:T(2,128)S(1)}) all-reduce(bf16[4,256,512]{1,2,0:T(8,128)(2,1)} %reduce-scatter.8.cloned.1.call-done, f32[2,2,512]{2,0,1:T(2,128)S(1)} %dynamic-slice_convert_fusion), channel_id=1, replica_groups=mesh['nodes'=16,'hid'=2] {'nodes'}, use_global_device_ids=true, to_apply=%region_14.15 | all-reduce | flops 526336 | bytes 3162112 | tf_op jit(solution)/shard_map/psum | solution.py:329
  528.3 5.1 psum.122
  534.0 3.4 divide_convert_fusion
  548.5 82.3 %all-reduce.22.cloned.1.call-done = (bf16[4,512,512]{2,1,0:T(8,128)(2,1)}, bf16[512,512]{1,0:T(8,128)(2,1)}, bf16[512,512]{1,0:T(8,128)(2,1)}) async-done(((bf16[4,512,512]{2,1,0:T(8,128)(2,1)}, bf16[512,512]{1,0:T(8,128)(2,1)}, bf16[512,512]{1,0:T(8,128)(2,1)}), (bf16[4,512,512]{2,1,0:T(8,128)(2,1)}, bf16[512,512]{1,0:T(8,128)(2,1)}, bf16[512,512]{1,0:T(8,128)(2,1)})) %all-reduce.22.cloned.1.call-update) | async-done | bytes 3145744 | tf_op jit(solution)/shard_map/psum | solution.py:366
  630.9 3.5 add_convert_fusion.7
  634.4 3.2 convolution_convert_fusion.11
  639.6 3.2 convolution_convert_fusion.15
  642.8 4.8 add_convert_fusion.15
  649.8 86.0 %all-reduce.20.cloned.1.call-done = (bf16[4,512,512]{2,1,0:T(8,128)(2,1)}, bf16[512,512]{1,0:T(8,128)(2,1)}, bf16[512,512]{1,0:T(8,128)(2,1)}) async-done(((bf16[4,512,512]{2,1,0:T(8,128)(2,1)}, bf16[512,512]{1,0:T(8,128)(2,1)}, bf16[512,512]{1,0:T(8,128)(2,1)}), (bf16[4,512,512]{2,1,0:T(8,128)(2,1)}, bf16[512,512]{1,0:T(8,128)(2,1)}, bf16[512,512]{1,0:T(8,128)(2,1)})) %all-reduce.20.cloned.1.call-update) | async-done | bytes 3145744 | tf_op jit(solution)/shard_map/psum | solution.py:366
  735.7 3.4 add_convert_fusion.6
  739.2 3.1 convolution_convert_fusion.10
  742.3 3.7 add_convert_fusion.10
  745.9 3.1 convolution_convert_fusion.14
  749.0 4.8 add_convert_fusion.14
  756.3 85.7 %all-reduce.18.cloned.1.call-done = (bf16[4,512,512]{2,1,0:T(8,128)(2,1)}, bf16[512,512]{1,0:T(8,128)(2,1)}, bf16[512,512]{1,0:T(8,128)(2,1)}) async-done(((bf16[4,512,512]{2,1,0:T(8,128)(2,1)}, bf16[512,512]{1,0:T(8,128)(2,1)}, bf16[512,512]{1,0:T(8,128)(2,1)}), (bf16[4,512,512]{2,1,0:T(8,128)(2,1)}, bf16[512,512]{1,0:T(8,128)(2,1)}, bf16[512,512]{1,0:T(8,128)(2,1)})) %all-reduce.18.cloned.1.call-update) | async-done | bytes 3145744 | tf_op jit(solution)/shard_map/psum | solution.py:366
  842.0 3.5 add_convert_fusion.5
  845.5 3.2 convolution_convert_fusion.9
  850.8 3.2 convolution_convert_fusion.13
  854.1 4.8 add_convert_fusion.13
  861.1 3.1 constant_dynamic-slice_fusion.1
  864.2 3.1 copy.206
  868.5 3.5 fusion.48
  872.0 3.2 copy.174
  878.2 68.9 %all-reduce.16.cloned.1.call-done = (bf16[4,512,512]{2,1,0:T(8,128)(2,1)}, bf16[512,512]{1,0:T(8,128)(2,1)}, bf16[512,512]{1,0:T(8,128)(2,1)}) async-done(((bf16[4,512,512]{2,1,0:T(8,128)(2,1)}, bf16[512,512]{1,0:T(8,128)(2,1)}, bf16[512,512]{1,0:T(8,128)(2,1)}), (bf16[4,512,512]{2,1,0:T(8,128)(2,1)}, bf16[512,512]{1,0:T(8,128)(2,1)}, bf16[512,512]{1,0:T(8,128)(2,1)})) %all-reduce.16.cloned.1.call-update) | async-done | bytes 3145744 | tf_op jit(solution)/shard_map/psum | solution.py:366
  947.1 5.4 multiply_subtract_fusion
  952.5 4.4 multiply_subtract_fusion.1
  956.9 7.1 multiply_subtract_fusion.2
  964.0 2.9 copy.176
  (275 shorter events, 99.9 us)
Async XLA Ops:
  7.2 165.0 %all-gather.3.cloned.1.call-start = ((), (), s32[]{:S(2)}) async-start(), calls=%async_computation.3 | async-start | bytes 2359296 | tf_op jit(solution)/shard_map/all_gather | solution.py:257
  8.8 3.8 copy-start.55
  9.1 3.5 copy-start.57
  11.6 5.6 copy-start.23
  16.2 7.2 copy-start.22
  17.2 18.9 %collective-permute-start = (bf16[2,192,512]{2,1,0:T(8,128)(2,1)}, bf16[2,192,512]{2,1,0:T(8,128)(2,1)S(1)}, u32[]{:S(2)}, u32[]{:S(2)}) collective-permute-start(bf16[2,192,512]{2,1,0:T(8,128)(2,1)} %get-tuple-element.150), channel_id=1, source_target_pairs={{0,1},{1,2},{2,3},{3,4},{4,5},{5,6},{6,7},{7,8},{8,9},{9,10},{10,1... | collective-permute-start | bytes 1179656 | tf_op jit(solution)/shard_map/ppermute | solution.py:41
  22.1 17.8 %collective-permute-start.1 = (bf16[2,192,512]{2,1,0:T(8,128)(2,1)}, bf16[2,192,512]{2,1,0:T(8,128)(2,1)}, u32[]{:S(2)}, u32[]{:S(2)}) collective-permute-start(bf16[2,192,512]{2,1,0:T(8,128)(2,1)} %get-tuple-element.151), channel_id=1, source_target_pairs={{1,0},{2,1},{3,2},{4,3},{5,4},{6,5},{7,6},{8,7},{9,8},{10,9},{11,1... | collective-permute-start | bytes 1179656 | tf_op jit(solution)/shard_map/ppermute | solution.py:43
  23.4 5.6 copy-start.62
  24.4 15.5 %slice-start.6 = ((bf16[3,768,512]{2,1,0:T(8,128)(2,1)}), bf16[2,768,512]{2,1,0:T(8,128)(2,1)S(1)}, s32[]{:S(2)}) async-start(bf16[3,768,512]{2,1,0:T(8,128)(2,1)} %copy-done.22), calls=%async_computation.19 | async-start | bytes 3145728 | tf_op jit(solution)/shard_map/slice | solution.py:236
  44.5 7.1 copy-start.20
  51.6 16.5 %copy-start.47 = (pred[768,16]{1,0:T(8,128)(4,1)S(1)}, pred[768,16]{1,0:T(8,128)(4,1)}, u32[]{:S(2)}) copy-start(pred[768,16]{1,0:T(8,128)(4,1)} %iota_compare_fusion.8) | copy-start | bytes 36868
  68.1 42.6 %copy-start.48 = (pred[768,16]{1,0:T(8,128)(4,1)S(1)}, pred[768,16]{1,0:T(8,128)(4,1)}, u32[]{:S(2)}) copy-start(pred[768,16]{1,0:T(8,128)(4,1)} %iota_compare_fusion.8) | copy-start | bytes 36868
  110.7 18.9 %copy-start.36 = (f32[768,4,16]{2,1,0:T(4,128)}, f32[768,4,16]{2,1,0:T(4,128)S(1)}, u32[]{:S(2)}) copy-start(f32[768,4,16]{2,1,0:T(4,128)S(1)} %get-tuple-element.161) | copy-start | bytes 589828
  113.6 16.0 %copy-start.38 = (f32[768,4]{1,0:T(8,128)}, f32[768,4]{1,0:T(8,128)S(1)}, u32[]{:S(2)}) copy-start(f32[768,4]{1,0:T(8,128)S(1)} %fusion.117) | copy-start | bytes 36868
  113.6 16.0 %copy-start.25 = (bf16[1,1152,512]{2,1,0:T(8,128)(2,1)S(1)}, bf16[1,1152,512]{2,1,0:T(8,128)(2,1)}, u32[]{:S(2)}) copy-start(bf16[1,1152,512]{2,1,0:T(8,128)(2,1)} %get-tuple-element.148) | copy-start | bytes 3538948
  130.8 6.0 copy-start.26
  130.8 6.0 copy-start.71
  143.6 57.3 %all-gather.5.cloned.1.call-start = ((), (), s32[]{:S(2)}) async-start(), calls=%async_computation.5 | async-start | bytes 2359296 | tf_op jit(solution)/shard_map/all_gather | solution.py:270
  144.3 101.2 %reduce-scatter.6.cloned.1.call-start = ((), (), s32[]{:S(2)}) async-start(), calls=%async_computation.6 | async-start | bytes 2359296 | tf_op jit(solution)/shard_map/reduce_scatter | solution.py:275
  200.9 8.7 copy-start.63
  212.7 55.1 %reduce-scatter.4.cloned.1.call-start = ((), (), s32[]{:S(2)}) async-start(), calls=%async_computation.4 | async-start | bytes 2359296 | tf_op jit(solution)/shard_map/reduce_scatter | solution.py:260
  218.3 201.4 %all-reduce.14.cloned.1.call-start = ((), (), s32[]{:S(2)}) async-start(), calls=%async_computation.8 | async-start | bytes 8388608 | tf_op jit(solution)/shard_map/psum | solution.py:329
  222.0 17.1 %copy-start.52 = (f32[768,4]{1,0:T(8,128)}, f32[768,4]{1,0:T(8,128)S(1)}, u32[]{:S(2)}) copy-start(f32[768,4]{1,0:T(8,128)S(1)} %log_add_fusion) | copy-start | bytes 36868
  222.0 17.1 %copy-start.64 = (bf16[1536,512]{0,1:T(8,128)(2,1)S(1)}, bf16[1536,512]{0,1:T(8,128)(2,1)}, u32[]{:S(2)}) copy-start(bf16[1536,512]{0,1:T(8,128)(2,1)} %all-gather.3.cloned.1.call-done) | copy-start | bytes 4718596
  222.0 17.1 %copy-start.77 = (bf16[1536,1024]{1,0:T(8,128)(2,1)S(1)}, bf16[1536,1024]{1,0:T(8,128)(2,1)}, u32[]{:S(2)}) copy-start(bf16[1536,1024]{1,0:T(8,128)(2,1)} %copy-done.76) | copy-start | bytes 9437188
  245.4 203.4 %reduce-scatter.8.cloned.1.call-start = ((), (), s32[]{:S(2)}) async-start(), calls=%async_computation.7 | async-start | bytes 3145728 | tf_op jit(solution)/shard_map/reduce_scatter | solution.py:321
  271.4 3.7 copy-start.27
  282.1 16.9 %copy-start.49 = (pred[768,16]{1,0:T(8,128)(4,1)S(1)}, pred[768,16]{1,0:T(8,128)(4,1)}, u32[]{:S(2)}) copy-start(pred[768,16]{1,0:T(8,128)(4,1)} %iota_compare_fusion.8) | copy-start | bytes 36868
  298.9 43.8 %copy-start.37 = (f32[768,4,16]{2,1,0:T(4,128)S(1)}, f32[768,4,16]{2,1,0:T(4,128)}, u32[]{:S(2)}) copy-start(f32[768,4,16]{2,1,0:T(4,128)} %copy-done.36) | copy-start | bytes 589828
  298.9 43.8 %copy-start.51 = (s32[768,16]{1,0:T(8,128)S(1)}, s32[768,16]{1,0:T(8,128)}, u32[]{:S(2)}) copy-start(s32[768,16]{1,0:T(8,128)} %copy.128) | copy-start | bytes 147460
  298.9 43.8 %copy-start.53 = (f32[768,4]{1,0:T(8,128)S(1)}, f32[768,4]{1,0:T(8,128)}, u32[]{:S(2)}) copy-start(f32[768,4]{1,0:T(8,128)} %copy-done.52) | copy-start | bytes 36868
  298.9 65.9 %slice-start.2 = ((s8[7077888]{0:T(1024)(128)(4,1)}), s8[2883584]{0:T(1024)(128)(4,1)S(1)}, s32[]{:S(2)}) async-start(s8[7077888]{0:T(1024)(128)(4,1)} %bitcast.179), calls=%async_computation.15 | async-start | bytes 5767168
  342.8 17.2 %copy-start.21 = (bf16[1,1152,512]{1,2,0:T(8,128)(2,1)S(1)}, bf16[1,1152,512]{1,2,0:T(8,128)(2,1)}, u32[]{:S(2)}) copy-start(bf16[1,1152,512]{1,2,0:T(8,128)(2,1)} %copy-done.20) | copy-start | bytes 3538948
  342.8 22.1 %slice-start.3 = ((s8[7077888]{0:T(1024)(128)(4,1)}), s8[4194304]{0:T(1024)(128)(4,1)S(1)}, s32[]{:S(2)}) async-start(s8[7077888]{0:T(1024)(128)(4,1)} %bitcast.179), calls=%async_computation.16 | async-start | bytes 8388608
  364.9 9.0 slice-start.4
  364.9 11.8 %slice-start = ((s8[7077888]{0:T(1024)(128)(4,1)}), s8[4194304]{0:T(1024)(128)(4,1)S(1)}, s32[]{:S(2)}) async-start(s8[7077888]{0:T(1024)(128)(4,1)} %bitcast.177), calls=%async_computation.13 | async-start | bytes 8388608
  366.3 7.6 slice-start.5
  366.3 10.5 %slice-start.1 = ((s8[7077888]{0:T(1024)(128)(4,1)}), s8[2883584]{0:T(1024)(128)(4,1)S(1)}, s32[]{:S(2)}) async-start(s8[7077888]{0:T(1024)(128)(4,1)} %bitcast.177), calls=%async_computation.14 | async-start | bytes 5767168
  387.2 7.0 copy-start.3
  387.2 7.0 copy-start.33
  387.2 7.6 copy-start.1
  390.1 4.7 copy-start
  390.2 16.2 %collective-permute-start.2 = (bf16[2,192,512]{2,1,0:T(8,128)(2,1)S(1)}, bf16[2,192,512]{2,1,0:T(8,128)(2,1)S(1)}, u32[]{:S(2)}, u32[]{:S(2)}) collective-permute-start(bf16[2,192,512]{2,1,0:T(8,128)(2,1)S(1)} %get-tuple-element.147), channel_id=1, source_target_pairs={{0,1},{1,2},{2,3},{3,4},{4,5},{5,6},{6,7},{7,8},{8,9},{9,10},{10,1... | collective-permute-start | bytes 1179656 | tf_op jit(solution)/shard_map/ppermute | solution.py:30
  392.7 18.4 %collective-permute-start.3 = (bf16[2,192,512]{2,1,0:T(8,128)(2,1)S(1)}, bf16[2,192,512]{2,1,0:T(8,128)(2,1)S(1)}, u32[]{:S(2)}, u32[]{:S(2)}) collective-permute-start(bf16[2,192,512]{2,1,0:T(8,128)(2,1)S(1)} %get-tuple-element.146), channel_id=1, source_target_pairs={{1,0},{2,1},{3,2},{4,3},{5,4},{6,5},{7,6},{8,7},{9,8},{10,9},{11,1... | collective-permute-start | bytes 1179656 | tf_op jit(solution)/shard_map/ppermute | solution.py:30
  415.5 215.4 %all-reduce.22.cloned.1.call-start = ((), (), s32[]{:S(2)}) async-start(), calls=%async_computation.12 | async-start | bytes 6291456 | tf_op jit(solution)/shard_map/psum | solution.py:366
  419.7 5.1 copy-start.17
  419.7 5.1 copy-start.35
  424.8 4.1 copy-start.24
  431.9 92.9 %copy-start.6 = (f32[4,256,512]{1,2,0:T(8,128)S(1)}, f32[4,256,512]{1,2,0:T(8,128)}, u32[]{:S(2)}) copy-start(f32[4,256,512]{1,2,0:T(8,128)} %copy.154) | copy-start | bytes 6291460
  541.4 4.0 copy-start.43
  548.5 82.4 %copy-start.42 = (bf16[1024,512]{1,0:T(8,128)(2,1)S(1)}, bf16[1024,512]{1,0:T(8,128)(2,1)}, u32[]{:S(2)}) copy-start(bf16[1024,512]{1,0:T(8,128)(2,1)} %copy-done.41) | copy-start | bytes 3145732
  548.5 187.2 %all-reduce.20.cloned.1.call-start = ((), (), s32[]{:S(2)}) async-start(), calls=%async_computation.11 | async-start | bytes 6291456 | tf_op jit(solution)/shard_map/psum | solution.py:366
  634.4 3.2 copy-start.67
  649.7 86.0 %copy-start.74 = (bf16[1024,512]{1,0:T(8,128)(2,1)S(1)}, bf16[1024,512]{1,0:T(8,128)(2,1)}, u32[]{:S(2)}) copy-start(bf16[1024,512]{1,0:T(8,128)(2,1)} %add_convert_fusion.7) | copy-start | bytes 3145732
  649.7 192.3 %all-reduce.18.cloned.1.call-start = ((), (), s32[]{:S(2)}) async-start(), calls=%async_computation.10 | async-start | bytes 6291456 | tf_op jit(solution)/shard_map/psum | solution.py:366
  756.0 86.1 %copy-start.75 = (bf16[1024,512]{1,0:T(8,128)(2,1)S(1)}, bf16[1024,512]{1,0:T(8,128)(2,1)}, u32[]{:S(2)}) copy-start(bf16[1024,512]{1,0:T(8,128)(2,1)} %add_convert_fusion.6) | copy-start | bytes 3145732
  756.0 191.1 %all-reduce.16.cloned.1.call-start = ((), (), s32[]{:S(2)}) async-start(), calls=%async_computation.9 | async-start | bytes 6291456 | tf_op jit(solution)/shard_map/psum | solution.py:366
  845.5 3.2 copy-start.69
  845.5 3.2 copy-start.73
  850.8 3.2 copy-start.31
  864.2 4.3 copy-start.4
  947.1 5.4 copy-start.66
  947.1 5.4 copy-start.72
  952.5 4.4 copy-start.29
  (36 other events, 76.7 us)
Sparse Core Ops, SparseCore 0:
  143.7 28.4 all-gather.2
  173.7 27.1 all-gather.4
  212.8 26.1 reduce-scatter.5
  241.6 26.1 reduce-scatter.3
  272.0 111.3 all-reduce.13
  415.6 33.1 reduce-scatter.7
  548.6 82.2 all-reduce.21
  649.8 85.8 all-reduce.19
  756.1 85.8 all-reduce.17
  861.2 85.8 all-reduce.15
where the time goes:
time: 981 us; the launch traced here: 974 us
  waiting for transfers between devices  426 us (43%)
  matrix products  307 us (31%)
  blocking collectives  86.4 us (9%)
  local copies, waits for them, and re-layouts  84.4 us (9%)
  other arithmetic  42.2 us (4%)
  between operations  16.3 us (2%)
  starting transfers between devices  11.5 us (1%)
    psum x4, waiting for transfers between devices, on_device(): lax.psum(part_attn.astype(jnp.bfloat16), 'hid').astype(jnp.float32)  323 us
    psum x1, blocking collectives, on_device(): lax.psum((attn_half, table_half, up_half, down_half), 'nodes')  76 us
    dot_general x1, matrix products, backward_block(): jnp.einsum('bkw,bhw->bhk', chooser, full_grads, precision=highest)  43.8 us
    dot_general x1, matrix products, attend(): jnp.einsum('bkw,bhw->bhk', chooser, full_scores, precision=highest)  42.6 us
    unnamed x181, local copies, waits for them, and re-layouts  29.9 us
    all_gather x1, waiting for transfers between devices, on_device(): inputs_all = lax.all_gather(second_in, 'hid', axis=0, tiled=True)  27.3 us
    dot_general x4, matrix products, schulz_update(): jnp.einsum('prc,pcd->prd', current_attn, poly_attn, preferred_element_typ...  21.6 us
    reduce_scatter x1, waiting for transfers between devices, on_device(): lax.psum_scatter(jnp.dot(activation, down_bf, preferred_element_type=jnp....  20.3 us
  transfers between devices with their start and end apart: 14, of which 12 were waited for; matrix products, arithmetic and copies ran while one was open for 21% of the time, Pallas kernels for 0%

commit v1 on v0

v1 whole, which is shorter than its diff:
```python
import functools
import math

import jax
import jax.numpy as jnp
from jax import lax
from jax.experimental import pallas as pl
from jax.experimental.pallas import tpu as pltpu
from jax.sharding import PartitionSpec as P

D = 512
HEADS = 4
HD = 128
FF = 2048
K = 16
NS_STEPS = 4
HALO = 192
BLOCK = 128
SPAN = BLOCK + 2 * HALO
RIM = 256
CHUNK = 512
TABLE_ROWS = 16

f32 = jnp.float32
bf16 = jnp.bfloat16
ns_first = 3.4445
ns_second = -4.775
ns_third = 2.0315
momentum_rate = 0.95
vector_rate = 0.9
muon_rate = 0.2
decay_rate = 0.1
score_scale = 1.0 / math.sqrt(HD)
AXES = ("nodes", "hid")
VMEM = pl.BlockSpec(memory_space=pltpu.VMEM)
SMEM = pl.BlockSpec(memory_space=pltpu.SMEM)


def nn(a, b):
    return lax.dot_general(a, b, (((1,), (0,)), ((), ())), preferred_element_type=f32)


def nt(a, b):
    return lax.dot_general(a, b, (((1,), (1,)), ((), ())), preferred_element_type=f32)


def tn(a, b):
    return lax.dot_general(a, b, (((0,), (0,)), ((), ())), preferred_element_type=f32)


def struct(shape, dtype):
    return jax.ShapeDtypeStruct(shape, dtype)


def rows_of(start, size):
    return pl.ds(pl.multiple_of(start, size), size)


def cost(flops, data):
    return pl.CostEstimate(flops=int(flops), bytes_accessed=int(data), transcendentals=0)


def norm_parts(field):
    average = jnp.mean(field, axis=-1, keepdims=True)
    centred = field - average
    variance = jnp.mean(centred * centred, axis=-1, keepdims=True)
    inverse = lax.rsqrt(variance + 1e-06)
    return centred * inverse, inverse


def table_rows(mod_ref, level, column):
    return jnp.where(level > 0.5, mod_ref[4 + column : 5 + column, :], mod_ref[column : column + 1, :])


def modulated(field, level, mod_ref, column):
    normed, _ = norm_parts(field)
    return normed * (1.0 + table_rows(mod_ref, level, column)) + table_rows(
        mod_ref, level, column + 1
    )


def norm_back(grad_out, field, level, mod_ref, column):
    normed, inverse = norm_parts(field)
    grad_norm = grad_out * (1.0 + table_rows(mod_ref, level, column))
    grad_in = inverse * (
        grad_norm
        - jnp.mean(grad_norm, axis=-1, keepdims=True)
        - normed * jnp.mean(grad_norm * normed, axis=-1, keepdims=True)
    )
    return grad_in, grad_out * normed


def add_table(table_ref, column, level, scale_term, shift_term):
    upper = level > 0.5
    for term, place in ((scale_term, column), (shift_term, column + 1)):
        low_part = jnp.sum(jnp.where(upper, 0.0, term), axis=0, keepdims=True)
        high_part = jnp.sum(jnp.where(upper, term, 0.0), axis=0, keepdims=True)
        table_ref[place : place + 1, :] += low_part
        table_ref[4 + place : 5 + place, :] += high_part


def slot_counts(pack, row_count, width, shift):
    pieces = []
    for left in range(0, width, 128):
        lanes = lax.broadcasted_iota(jnp.int32, (row_count, 128), 1)
        rows = lax.broadcasted_iota(jnp.int32, (row_count, 128), 0)
        place = (lanes - rows + (left - shift)).astype(f32)
        total = jnp.zeros((row_count, 128), f32)
        for slot in range(K):
            total = total + jnp.where(place == pack[:, slot : slot + 1], 1.0, 0.0)
        pieces.append(total)
    return jnp.concatenate(pieces, axis=1).astype(bf16)


def project_kernel(features, pack, mod, weights, first_in, qkv, counts):
    blocks = features.shape[0] // BLOCK

    def step(b, carry):
        rows = rows_of(b * BLOCK, BLOCK)
        level = pack[rows, K : K + 1]
        first_in[rows, :] = modulated(features[rows, :].astype(f32), level, mod, 0).astype(bf16)
        return carry

    lax.fori_loop(0, blocks, step, 0)
    for p in range(3):
        qkv[p] = nn(first_in[...], weights[p]).astype(bf16)

    def count_step(b, carry):
        rows = rows_of(b * BLOCK, BLOCK)
        counts[rows, :] = slot_counts(pack[rows, :], BLOCK, SPAN, HALO)
        return carry

    lax.fori_loop(0, blocks, count_step, 0)


def forward_kernel(
    rim_low,
    rim_high,
    features,
    pack,
    mod,
    weights,
    qkv,
    counts,
    attended,
    stream,
    second_in,
    padded,
    rim_queries,
    rim_counts,
    log_totals,
    rim_in,
):
    row_count = features.shape[0]
    for side, rim in enumerate((rim_low, rim_high)):
        for start in range(0, HALO, 64):
            rows = slice(start, start + 64)
            info = rim[rows, D:].astype(f32)
            rim_in[side * HALO + start : side * HALO + start + 64, :] = modulated(
                rim[rows, :D].astype(f32), info[:, K : K + 1], mod, 0
            ).astype(bf16)
            rim_counts[side * HALO + start : side * HALO + start + 64, :] = slot_counts(
                info, 64, RIM, start + (-HALO if side == 0 else RIM)
            )
    rim_queries[...] = nn(rim_in[...], weights[0]).astype(bf16)
    for p in range(2):
        piece = nn(rim_in[...], weights[1 + p]).astype(bf16)
        padded[p, :HALO, :] = piece[:HALO]
        padded[p, HALO + row_count :, :] = piece[HALO:]
        padded[p, HALO : HALO + row_count, :] = qkv[1 + p]

    def step(b, carry):
        rows = rows_of(b * BLOCK, BLOCK)
        span = pl.ds(pl.multiple_of(b * BLOCK, BLOCK), SPAN)
        count = counts[rows, :].astype(f32)
        live = count > 0.0
        lanes = lax.broadcasted_iota(jnp.int32, (BLOCK, 128), 1)
        stats = jnp.zeros((BLOCK, 128), f32)
        for h in range(HEADS):
            cols = slice(h * HD, (h + 1) * HD)
            scores = nt(qkv[0, rows, cols], padded[0, span, cols]) * score_scale
            masked = jnp.where(live, scores, -1e30)
            peak = jnp.max(masked, axis=-1, keepdims=True)
            exponent = jnp.exp(masked - peak)
            total = jnp.sum(exponent * count, axis=-1, keepdims=True)
            probs = (exponent / total).astype(bf16)
            spread = (probs.astype(f32) * count).astype(bf16)
            attended[rows, cols] = nn(spread, padded[1, span, cols]).astype(bf16)
            stats = jnp.where(lanes == h, peak + jnp.log(total), stats)
        log_totals[rows, :] = stats
        return carry

    lax.fori_loop(0, row_count // BLOCK, step, 0)

    def tail(b, carry):
        rows = rows_of(b * 256, 256)
        field = features[rows, :].astype(f32) + nn(attended[rows, :], weights[3])
        stream[rows, :] = field
        second_in[rows, :] = modulated(field, pack[rows, K : K + 1], mod, 2).astype(bf16)
        return carry

    lax.fori_loop(0, row_count // 256, tail, 0)


def mlp_chunk(scalars, second_in, cotangent, up, down, branch, grad_second, acts, grads, out_up, out_down):
    row_count = second_in.shape[0]

    def step(b, carry):
        rows = rows_of(b * 256, 256)
        preact = nn(second_in[rows, :], up)
        sigmoid = 1.0 / (1.0 + jnp.exp(-preact))
        act = (preact * sigmoid).astype(bf16)
        acts[rows, :] = act
        branch[rows, :] += nn(act, down)
        grad_act = nt(cotangent[rows, :], down)
        grad_pre = (grad_act * (sigmoid * (1.0 + preact * (1.0 - sigmoid)))).astype(bf16)
        grads[rows, :] = grad_pre
        grad_second[rows, :] += nt(grad_pre, up)
        return carry

    lax.fori_loop(0, row_count // 256, step, 0)
    z1, z2 = scalars[2], scalars[3]
    for left, right, out in ((second_in, grads, out_up), (cotangent, acts, out_down)):
        product = tn(left[...], right[...])
        for q in range(4):
            out[0, (q // 2) ^ z1, (q % 2) ^ z2] = product[q * 128 : (q + 1) * 128].astype(bf16)


def mlp_own_kernel(
    scalars, second_in, cotangent, up, down, branch, grad_second, out_up, out_down, acts, grads
):
    @pl.when(pl.program_id(0) == 0)
    def _():
        branch[...] = jnp.zeros_like(branch)
        grad_second[...] = jnp.zeros_like(grad_second)

    mlp_chunk(
        scalars,
        second_in,
        cotangent,
        up[...].astype(bf16),
        down[...].astype(bf16),
        branch,
        grad_second,
        acts,
        grads,
        out_up,
        out_down,
    )


def mlp_rest_kernel(
    scalars,
    second_in,
    cotangent,
    near,
    far,
    branch_in,
    grad_in,
    stream,
    pack,
    mod,
    weights,
    attended,
    log_totals,
    out_up,
    out_down,
    output,
    grad_stream,
    grad_attended,
    stats,
    edge_low,
    edge_high,
    table,
    branch,
    grad_second,
    acts,
    grads,
):
    row_count = second_in.shape[0]
    turn = pl.program_id(0)

    @pl.when(turn == 0)
    def _():
        branch[...] = branch_in[...]
        grad_second[...] = grad_in[...]
        mlp_chunk(
            scalars, second_in, cotangent, near[0], near[1], branch, grad_second, acts, grads, out_up, out_down
        )

    @pl.when(turn == 1)
    def _():
        mlp_chunk(
            scalars, second_in, cotangent, far[0], far[1], branch, grad_second, acts, grads, out_up, out_down
        )
        table[...] = jnp.zeros_like(table)

        def step(b, carry):
            rows = rows_of(b * BLOCK, BLOCK)
            field = stream[rows, :]
            level = pack[rows, K : K + 1]
            output[rows, :] = (field + branch[rows, :]).astype(bf16)
            gradient = grad_second[rows, :]
            grad_field, scale_term = norm_back(gradient, field, level, mod, 2)
            add_table(table, 2, level, scale_term, gradient)
            total = cotangent[rows, :].astype(f32) + grad_field
            grad_stream[rows, :] = total
            back = nt(total.astype(bf16), weights[3]).astype(bf16)
            grad_attended[rows, :] = back
            product = back.astype(f32) * attended[rows, :].astype(f32)
            lanes = lax.broadcasted_iota(jnp.int32, (BLOCK, 128), 1)
            kept = log_totals[rows, :]
            for h in range(HEADS):
                delta = jnp.sum(product[:, h * HD : (h + 1) * HD], axis=-1, keepdims=True)
                kept = jnp.where(lanes == HEADS + h, delta, kept)
            stats[rows, :] = kept
            return carry

        lax.fori_loop(0, row_count // BLOCK, step, 0)
        for edge, first in ((edge_low, 0), (edge_high, row_count - HALO)):
            rows = slice(first, first + HALO)
            edge[:, :D] = grad_attended[rows, :]
            kept = stats[rows, :]
            upper = kept.astype(bf16)
            lower = (kept - upper.astype(f32)).astype(bf16).astype(f32)
            edge[:, D:] = (upper.astype(f32) + pltpu.roll(lower, 2 * HEADS, 1)).astype(bf16)


def attention_terms(query, key, value, grad, count, log_total, delta):
    scores = nt(query, key) * score_scale
    probs = jnp.exp(jnp.where(count > 0.0, scores, -1e30) - log_total)
    grad_probs = nt(grad, value)
    slopes = (probs * (grad_probs - delta)).astype(bf16).astype(f32)
    spread = (probs.astype(bf16).astype(f32) * count).astype(bf16)
    return (slopes * count).astype(bf16), spread


def backward_kernel(
    head,
    query,
    padded,
    grad,
    stats,
    counts,
    rim_query,
    rim_counts,
    grad_low,
    info_low,
    grad_high,
    info_high,
    grad_query,
    grad_key,
    grad_value,
    keys_total,
    values_total,
):
    row_count = query.shape[1]
    keys_total[...] = jnp.zeros_like(keys_total)
    values_total[...] = jnp.zeros_like(values_total)

    def step(b, carry):
        rows = rows_of(b * BLOCK, BLOCK)
        span = pl.ds(pl.multiple_of(b * BLOCK, BLOCK), SPAN)
        slopes, spread = attention_terms(
            query[0, rows, :],
            padded[0, span, :],
            padded[1, span, :],
            grad[rows, :],
            counts[rows, :].astype(f32),
            stats[rows, head : head + 1],
            stats[rows, HEADS + head : HEADS + head + 1],
        )
        grad_query[rows, :] = (nn(slopes, padded[0, span, :]) * score_scale).astype(bf16)
        keys_total[span, :] += tn(slopes, query[0, rows, :])
        values_total[span, :] += tn(spread, grad[rows, :])
        return carry

    lax.fori_loop(0, row_count // BLOCK, step, 0)
    for side, (grads, info) in enumerate(((grad_low, info_low), (grad_high, info_high))):
        first = HALO if side == 0 else HALO + row_count - RIM
        span = slice(first, first + RIM)
        rows = slice(side * HALO, (side + 1) * HALO)
        known = info[...].astype(f32)
        log_total = known[:, head : head + 1] + known[:, 2 * HEADS + head : 2 * HEADS + head + 1]
        delta = known[:, HEADS + head : HEADS + head + 1] + known[:, 3 * HEADS + head : 3 * HEADS + head + 1]
        slopes, spread = attention_terms(
            rim_query[rows, :],
            padded[0, span, :],
            padded[1, span, :],
            grads[...],
            rim_counts[rows, :].astype(f32),
            log_total,
            delta,
        )
        keys_total[span, :] += tn(slopes, rim_query[rows, :])
        values_total[span, :] += tn(spread, grads[...])
    own = slice(HALO, HALO + row_count)
    grad_key[...] = (keys_total[own, :] * score_scale).astype(bf16)
    grad_value[...] = values_total[own, :].astype(bf16)


def weights_kernel(*refs):
    scalars = refs[0]
    pieces = refs[1 : 1 + 3 * HEADS]
    (first_in, attended, grad_stream, features, pack, mod, weights, table_two, features_grad, blocks, gathered, table) = refs[
        1 + 3 * HEADS :
    ]
    row_count = first_in.shape[0]
    for p in range(3):
        for h in range(HEADS):
            gathered[p, :, h * HD : (h + 1) * HD] = pieces[p * HEADS + h][...]
    table[...] = table_two[...]

    def step(b, carry):
        rows = rows_of(b * 256, 256)
        level = pack[rows, K : K + 1]
        gradient = nt(gathered[0, rows, :], weights[0])
        for p in range(1, 3):
            gradient = gradient + nt(gathered[p, rows, :], weights[p])
        grad_field, scale_term = norm_back(gradient, features[rows, :].astype(f32), level, mod, 0)
        add_table(table, 0, level, scale_term, gradient)
        total = grad_stream[rows, :]
        features_grad[rows, :] = total + grad_field
        gathered[3, rows, :] = total.astype(bf16)
        return carry

    lax.fori_loop(0, row_count // 256, step, 0)
    core, slot_bit, z1, z2, hid = (scalars[i] for i in range(5))
    for p in range(4):
        left = first_in if p < 3 else attended
        product = tn(left[...], gathered[p])
        target, slot = p // 2, p % 2
        for half in range(2):
            for q in range(4):
                index = block_index(target, 2, slot ^ slot_bit, half ^ hid, (q // 2) ^ z1, (q % 2) ^ z2)
                start = half * 256 + q * 64
                where_to = (target ^ core,) + tuple(index)
                blocks[where_to + (slice(0, 64),)] = product[start : start + 64].astype(bf16)
                if p == 0:
                    row = (q // 2) * 4 + 2 * half + q % 2
                    extra = jnp.broadcast_to(table[row : row + 1, :], (TABLE_ROWS, D))
                    blocks[where_to + (slice(64, 80),)] = extra.astype(bf16)
                else:
                    blocks[where_to + (slice(64, 80),)] = jnp.zeros((TABLE_ROWS, D), bf16)


def block_index(target, phase, slot, hid, row_half, row_quarter):
    if phase == 1:
        return (slot, hid, row_half, row_quarter) if target == 0 else (row_half, slot, hid, row_quarter)
    return (hid, slot, row_half, row_quarter) if target == 0 else (slot, row_half, hid, row_quarter)


def newton_schulz(read, write, scratch, parts, rows_first, scale):
    squared = scale * scale
    grams = []
    for half in range(2):
        total = None
        for part in parts[half]:
            block = read(part)
            term = tn(block, block) if rows_first else nt(block, block)
            total = term if total is None else total + term
        grams.append((total * squared).astype(bf16))
    gram = (grams[0].astype(f32) + grams[1].astype(f32)).astype(bf16)
    scratch[...] = (ns_second * gram.astype(f32) + ns_third * nn(gram, gram)).astype(bf16)
    for half in range(2):
        for part in parts[half]:
            block = read(part)
            other = nn(block, scratch[...]) if rows_first else nn(scratch[...], block)
            write(part, ((ns_first * block.astype(f32) + other) * scale).astype(bf16))


def large_kernel(scalars, kept, got, result, blend, work, poly):
    core, slot_bit, z1, z2 = (scalars[i] for i in range(4))
    total = jnp.zeros((8, D), f32)
    for n in range(16):
        b1, b2, b3, b4 = n // 8, (n // 4) % 2, (n // 2) % 2, n % 2
        source = kept if b1 == 0 else got
        block = source[b2, b3, b4]
        value = block.astype(f32)
        total = total + jnp.sum((value * value).reshape(16, 8, D), axis=0)
        slot = jnp.where(core == 0, b1, b2)
        half = jnp.where(core == 0, b2, b3)
        row_half = jnp.where(core == 0, b3, b1)
        start = ((row_half ^ z1) * 2 + (b4 ^ z2)) * 128
        work[half * 2 + (slot ^ slot_bit), rows_of(start, 128), :] = block
    scale = 1.0 / (jnp.sqrt(jnp.sum(total)) + 1e-07)
    for s in range(2):
        blend[s] = work[s]

    def write(part, value):
        work[part] = value

    def step(i, factor):
        newton_schulz(lambda part: work[part], write, poly, ((0, 1), (2, 3)), False, factor)
        return jnp.ones((), f32)

    lax.fori_loop(0, NS_STEPS, step, scale)
    for s in range(2):
        result[s] = work[s]


def small_kernel(scalars, kept, got, result, work, poly):
    core, slot_bit, z1, z2 = (scalars[i] for i in range(4))
    totals = [jnp.zeros((8, D), f32), jnp.zeros((8, D), f32)]
    for n in range(16):
        b1, b2, b3, b4 = n // 8, (n // 4) % 2, (n // 2) % 2, n % 2
        source = kept if b1 == 0 else got
        block = source[b2, b3, b4]
        rows = block[:64]
        slot = jnp.where(core == 0, b2, b1) ^ slot_bit
        half = jnp.where(core == 0, b1, b3)
        row_half = jnp.where(core == 0, b3, b2)
        quarter = (row_half ^ z1) * 2 + (b4 ^ z2)
        work[slot, half, rows_of(quarter * 64, 64), :] = rows

        @pl.when((half == 0) & (slot == 0))
        def _():
            result[4, rows_of(quarter * TABLE_ROWS, TABLE_ROWS), :] = block[64:]

    result[4, 64:, :] = jnp.zeros((192, D), bf16)
    for s in range(2):
        total = jnp.zeros((8, D), f32)
        for half in range(2):
            value = work[s, half].astype(f32)
            total = total + jnp.sum((value * value).reshape(32, 8, D), axis=0)
        scale = 1.0 / (jnp.sqrt(jnp.sum(total)) + 1e-07)
        result[2 + s] = work[s, 0]

        def write(part, value):
            work[s, part] = value

        def step(i, factor):
            newton_schulz(lambda part: work[s, part], write, poly, ((0,), (1,)), True, factor)
            return jnp.ones((), f32)

        lax.fori_loop(0, NS_STEPS, step, scale)
        result[s] = work[s, 0]


def new_moment(blend, moment):
    share = 1.0 / (1.0 + momentum_rate)
    return share * blend + (momentum_rate - share * momentum_rate * momentum_rate) * moment


def new_weight(weight, ortho, longest):
    return weight - muon_rate * (0.2 * math.sqrt(longest) * ortho + decay_rate * weight)


def large_out_kernel(
    scalars, own, got, up_weight, up_moment, down_weight, down_moment, up_moment_new, up_new, down_moment_new, down_new
):
    first = scalars[0] == 0
    ups = [jnp.where(first, own[i, 0].astype(f32), got[i, 0].astype(f32)) for i in range(2)]
    downs = [jnp.where(first, got[i, 0].astype(f32), own[i, 0].astype(f32)) for i in range(2)]
    up_new[...] = new_weight(up_weight[...], ups[0], FF)
    up_moment_new[...] = new_moment(ups[1], up_moment[...])
    down_new[...] = new_weight(down_weight[...], downs[0].T, FF)
    down_moment_new[...] = new_moment(downs[1].T, down_moment[...])


def small_out_kernel(scalars, own, got, weight, moment, moment_new, weight_new):
    mine = scalars[0] == pl.program_id(0) // 2
    ortho = jnp.where(mine, own[0, 0].astype(f32), got[0, 0].astype(f32))
    blend = jnp.where(mine, own[1, 0].astype(f32), got[1, 0].astype(f32))
    weight_new[0] = new_weight(weight[0], ortho, D)
    moment_new[0] = new_moment(blend, moment[0])


def on_device(
    features,
    levels,
    neighbour_index,
    neighbour_count,
    cotangent,
    attention_weight,
    up_weight,
    down_weight,
    modulation,
    attention_moment,
    up_moment,
    down_moment,
    modulation_moment,
):
    row_count = features.shape[0]
    device_count = lax.axis_size(AXES)
    me = lax.axis_index(AXES)
    first_row = me * row_count

    def bit(mask):
        return (me // mask) % 2

    hid, core, slot_bit, z1, z2 = bit(1), bit(2), bit(4), bit(8), bit(16)
    scalars = jnp.stack([core, slot_bit, z1, z2, hid]).astype(jnp.int32)
    is_first = core == 0

    def along(value, distance):
        pairs = [(i, i + distance) for i in range(device_count) if 0 <= i + distance < device_count]
        return lax.ppermute(value, AXES, pairs)

    def swap(value, mask, other=None):
        masks = (mask, mask if other is None else other)
        pairs = [(i, i ^ masks[(i // 2) % 2]) for i in range(device_count)]
        return lax.ppermute(value, AXES, pairs)

    live = jnp.arange(K, dtype=jnp.int32)[None, :] < neighbour_count[:, None]
    row_ids = first_row + jnp.arange(row_count, dtype=jnp.int32)[:, None]
    offsets = jnp.where(live, neighbour_index - row_ids, 512)
    pack = jnp.concatenate(
        [offsets, levels[:, None], jnp.zeros((row_count, 128 - K - 1), jnp.int32)], axis=1
    ).astype(f32)
    rims = jnp.concatenate([features, pack.astype(bf16)], axis=1)
    rim_low = along(rims[row_count - HALO :], 1)
    rim_high = along(rims[:HALO], -1)
    quarter = jnp.stack(
        [
            lax.dynamic_slice(up_weight, (0, core * CHUNK), (D, CHUNK)),
            lax.dynamic_slice(down_weight, (core * CHUNK, 0), (CHUNK, D)),
        ]
    ).astype(bf16)
    near = swap(quarter, 1)
    far = swap(near, 2)

    attn_bf = attention_weight.astype(bf16)
    mod = modulation.reshape(8, D)
    first_in, qkv, counts = pl.pallas_call(
        project_kernel,
        out_shape=(
            struct((row_count, D), bf16),
            struct((3, row_count, D), bf16),
            struct((row_count, SPAN), bf16),
        ),
        in_specs=[VMEM] * 4,
        out_specs=(VMEM,) * 3,
        cost_estimate=cost(4e9, 4e6),
        name="project",
    )(features, pack, mod, attn_bf)

    attended, stream, second_in, padded, rim_queries, rim_counts, log_totals = pl.pallas_call(
        forward_kernel,
        out_shape=(
            struct((row_count, D), bf16),
            struct((row_count, D), f32),
            struct((row_count, D), bf16),
            struct((2, row_count + 2 * HALO, D), bf16),
            struct((2 * HALO, D), bf16),
            struct((2 * HALO, RIM), bf16),
            struct((row_count, 128), f32),
        ),
        in_specs=[VMEM] * 8,
        out_specs=(VMEM,) * 7,
        scratch_shapes=[pltpu.VMEM((2 * HALO, D), bf16)],
        cost_estimate=cost(6e9, 8e6),
        name="attend",
    )(rim_low, rim_high, features, pack, mod, attn_bf, qkv, counts)

    def whole(*shape):
        return pl.BlockSpec(shape, lambda g, s: (0,) * len(shape))

    chunk_shape = struct((2, 2, 2, 128, CHUNK), bf16)
    branch, grad_second, own_up, own_down = pl.pallas_call(
        mlp_own_kernel,
        out_shape=(struct((row_count, D), f32), struct((row_count, D), f32), chunk_shape, chunk_shape),
        grid_spec=pltpu.PrefetchScalarGridSpec(
            num_scalar_prefetch=1,
            grid=(2,),
            in_specs=[
                whole(row_count, D),
                whole(row_count, D),
                pl.BlockSpec((D, CHUNK), lambda g, s: (0, g)),
                pl.BlockSpec((CHUNK, D), lambda g, s: (g, 0)),
            ],
            out_specs=(
                whole(row_count, D),
                whole(row_count, D),
                pl.BlockSpec((1, 2, 2, 128, CHUNK), lambda g, s: (g ^ s[1], 0, 0, 0, 0)),
                pl.BlockSpec((1, 2, 2, 128, CHUNK), lambda g, s: (g ^ s[1], 0, 0, 0, 0)),
            ),
            scratch_shapes=[pltpu.VMEM((row_count, CHUNK), bf16)] * 2,
        ),
        cost_estimate=cost(5e9, 8e6),
        name="mlp_own",
    )(scalars, second_in, cotangent, up_weight, down_weight)

    (
        rest_up,
        rest_down,
        output,
        grad_stream,
        grad_attended,
        stats,
        edge_low,
        edge_high,
        table_two,
    ) = pl.pallas_call(
        mlp_rest_kernel,
        out_shape=(
            chunk_shape,
            chunk_shape,
            struct((row_count, D), bf16),
            struct((row_count, D), f32),
            struct((row_count, D), bf16),
            struct((row_count, 128), f32),
            struct((HALO, D + 128), bf16),
            struct((HALO, D + 128), bf16),
            struct((8, D), f32),
        ),
        grid_spec=pltpu.PrefetchScalarGridSpec(
            num_scalar_prefetch=1,
            grid=(2,),
            in_specs=[
                whole(row_count, D),
                whole(row_count, D),
                whole(2, D, CHUNK),
                whole(2, D, CHUNK),
                whole(row_count, D),
                whole(row_count, D),
                whole(row_count, D),
                whole(row_count, 128),
                whole(8, D),
                whole(4, D, D),
                whole(row_count, D),
                whole(row_count, 128),
            ],
            out_specs=(
                pl.BlockSpec((1, 2, 2, 128, CHUNK), lambda g, s: (g ^ s[0] ^ s[1], 0, 0, 0, 0)),
                pl.BlockSpec((1, 2, 2, 128, CHUNK), lambda g, s: (g ^ s[0] ^ s[1], 0, 0, 0, 0)),
                whole(row_count, D),
                whole(row_count, D),
                whole(row_count, D),
                whole(row_count, 128),
                whole(HALO, D + 128),
                whole(HALO, D + 128),
                whole(8, D),
            ),
            scratch_shapes=[
                pltpu.VMEM((row_count, D), f32),
                pltpu.VMEM((row_count, D), f32),
                pltpu.VMEM((row_count, CHUNK), bf16),
                pltpu.VMEM((row_count, CHUNK), bf16),
            ],
        ),
        cost_estimate=cost(6e9, 12e6),
        name="mlp_rest",
    )(
        scalars,
        second_in,
        cotangent,
        near,
        far,
        branch,
        grad_second,
        stream,
        pack,
        mod,
        attn_bf,
        attended,
        log_totals,
    )

    grad_low = along(edge_high, 1)
    grad_high = along(edge_low, -1)

    def kept_of(first, second):
        return jnp.where(is_first, first, second)

    own_sum = kept_of(own_up, own_down).astype(f32) + swap(kept_of(own_down, own_up), 2).astype(f32)
    rest_sum = kept_of(rest_up, rest_down).astype(f32) + swap(kept_of(rest_down, rest_up), 2).astype(f32)

    def halved(first_send, first_keep, routes):
        keep, send = first_keep, first_send
        for number, route in enumerate(routes):
            keep = keep + swap(send.astype(bf16), *route).astype(f32)
            if number + 1 < len(routes):
                keep, send = keep[0], keep[1]
        mask = 32
        while mask < device_count:
            rounded = keep.astype(bf16)
            keep = rounded.astype(f32) + swap(rounded, mask).astype(f32)
            mask *= 2
        return keep

    def doubled(shard, routes):
        pieces = shard
        for route in routes[:0:-1]:
            pieces = jnp.stack([pieces, swap(pieces, *route)])
        return pieces, swap(pieces, *routes[0])

    blend_rate = 1.0 + momentum_rate
    past_rate = momentum_rate * momentum_rate
    large_routes = ((4, 8), (1, 4), (8, 1), (16, 16))
    large_keep = kept_of(
        jnp.stack([own_sum[0], rest_sum[0]]),
        jnp.stack([own_sum[:, 0], rest_sum[:, 0]], axis=1),
    )
    large_send = kept_of(
        jnp.stack([own_sum[1], rest_sum[1]]),
        jnp.stack([own_sum[:, 1], rest_sum[:, 1]], axis=1),
    )
    large_shard = halved(large_send, large_keep, large_routes)
    row_start = (z1 * 2 + z2) * 128
    large_past = kept_of(
        lax.dynamic_slice(up_moment, (row_start, slot_bit * CHUNK), (128, CHUNK)),
        lax.dynamic_slice(down_moment, (slot_bit * CHUNK, row_start), (CHUNK, 128)).T,
    )
    large_blend = (blend_rate * large_shard + past_rate * large_past).astype(bf16)
    large_kept, large_got = doubled(large_blend, large_routes)

    def column(h):
        return pl.BlockSpec((row_count, HD), lambda g: (0, h))

    pieces = []
    for h in range(HEADS):
        pieces.append(
            pl.pallas_call(
                functools.partial(backward_kernel, h),
                grid=(1,),
                out_shape=(struct((row_count, HD), bf16),) * 3,
                in_specs=[
                    pl.BlockSpec((1, row_count, HD), lambda g, h=h: (0, 0, h)),
                    pl.BlockSpec((2, row_count + 2 * HALO, HD), lambda g, h=h: (0, 0, h)),
                    pl.BlockSpec((row_count, HD), lambda g, h=h: (0, h)),
                    pl.BlockSpec((row_count, 128), lambda g: (0, 0)),
                    pl.BlockSpec((row_count, SPAN), lambda g: (0, 0)),
                    pl.BlockSpec((2 * HALO, HD), lambda g, h=h: (0, h)),
                    pl.BlockSpec((2 * HALO, RIM), lambda g: (0, 0)),
                    pl.BlockSpec((HALO, HD), lambda g, h=h: (0, h)),
                    pl.BlockSpec((HALO, 128), lambda g: (0, HEADS)),
                    pl.BlockSpec((HALO, HD), lambda g, h=h: (0, h)),
                    pl.BlockSpec((HALO, 128), lambda g: (0, HEADS)),
                ],
                out_specs=(pl.BlockSpec((row_count, HD), lambda g: (0, 0)),) * 3,
                scratch_shapes=[pltpu.VMEM((row_count + 2 * HALO, HD), f32)] * 2,
                cost_estimate=cost(1e9, 3e6),
                name="attend_back",
            )(
                qkv,
                padded,
                grad_attended,
                stats,
                counts,
                rim_queries,
                rim_counts,
                grad_low,
                grad_low,
                grad_high,
                grad_high,
            )
        )
    ordered = [pieces[h][p] for p in range(3) for h in range(HEADS)]
    features_grad, attn_blocks = pl.pallas_call(
        weights_kernel,
        out_shape=(struct((row_count, D), f32), struct((2, 2, 2, 2, 2, 80, D), bf16)),
        in_specs=[SMEM] + [VMEM] * (3 * HEADS + 8),
        out_specs=(VMEM, VMEM),
        scratch_shapes=[pltpu.VMEM((4, row_count, D), bf16), pltpu.VMEM((8, D), f32)],
        cost_estimate=cost(4e9, 9e6),
        name="attend_weights",
    )(
        scalars,
        *ordered,
        first_in,
        attended,
        grad_stream,
        features,
        pack,
        mod,
        attn_bf,
        table_two,
    )

    small_routes = ((1, 4), (4, 8), (8, 1), (16, 16))
    small_sum = attn_blocks[0].astype(f32) + swap(attn_blocks[1], 2).astype(f32)
    small_shard = halved(small_sum[1], small_sum[0], small_routes)
    small_past = lax.dynamic_slice(
        attention_moment, (core * 2 + slot_bit, (z1 * 2 + z2) * 64, 0), (1, 64, D)
    )[0]
    small_blend = jnp.concatenate(
        [
            (blend_rate * small_shard[:64] + past_rate * small_past).astype(bf16),
            small_shard[64:].astype(bf16),
        ]
    )
    small_kept, small_got = doubled(small_blend, small_routes)

    large_result, large_mix = pl.pallas_call(
        large_kernel,
        out_shape=(struct((2, D, CHUNK), bf16), struct((2, D, CHUNK), bf16)),
        in_specs=[SMEM, VMEM, VMEM],
        out_specs=(VMEM, VMEM),
        scratch_shapes=[pltpu.VMEM((4, D, CHUNK), bf16), pltpu.VMEM((D, D), bf16)],
        cost_estimate=cost(1e10, 6e6),
        name="ortho_large",
    )(scalars, large_kept, large_got)
    large_own = jnp.stack([large_result, large_mix])
    large_other = swap(large_own, 2)
    up_moment_new, up_new, down_moment_new, down_new = pl.pallas_call(
        large_out_kernel,
        grid=(2,),
        out_shape=(struct((D, 2 * CHUNK), f32),) * 2 + (struct((2 * CHUNK, D), f32),) * 2,
        in_specs=[
            SMEM,
            pl.BlockSpec((2, 1, D, CHUNK), lambda g: (0, g, 0, 0)),
            pl.BlockSpec((2, 1, D, CHUNK), lambda g: (0, g, 0, 0)),
            pl.BlockSpec((D, CHUNK), lambda g: (0, g)),
            pl.BlockSpec((D, CHUNK), lambda g: (0, g)),
            pl.BlockSpec((CHUNK, D), lambda g: (g, 0)),
            pl.BlockSpec((CHUNK, D), lambda g: (g, 0)),
        ],
        out_specs=(
            pl.BlockSpec((D, CHUNK), lambda g: (0, g)),
            pl.BlockSpec((D, CHUNK), lambda g: (0, g)),
            pl.BlockSpec((CHUNK, D), lambda g: (g, 0)),
            pl.BlockSpec((CHUNK, D), lambda g: (g, 0)),
        ),
        cost_estimate=cost(1e7, 2e7),
        name="update_large",
    )(scalars, large_own, large_other, up_weight, up_moment, down_weight, down_moment)

    small_own = pl.pallas_call(
        small_kernel,
        out_shape=struct((5, 256, D), bf16),
        in_specs=[SMEM, VMEM, VMEM],
        out_specs=VMEM,
        scratch_shapes=[pltpu.VMEM((2, 2, 256, D), bf16), pltpu.VMEM((D, D), bf16)],
        cost_estimate=cost(6e9, 4e6),
        name="ortho_small",
    )(scalars, small_kept, small_got)
    small_other = swap(small_own, 2)

    def pair(g, s):
        return (0, g % 2, 0, 0)

    def per_matrix(index):
        return pl.BlockSpec((1, 256, D), index)

    attention_moment_new, attention_new = pl.pallas_call(
        small_out_kernel,
        grid_spec=pltpu.PrefetchScalarGridSpec(
            num_scalar_prefetch=1,
            grid=(4,),
            in_specs=[
                pl.BlockSpec((2, 1, 256, D), pair),
                pl.BlockSpec((2, 1, 256, D), pair),
                per_matrix(lambda g, s: (g, s[4], 0)),
                per_matrix(lambda g, s: (g, 0, 0)),
            ],
            out_specs=(per_matrix(lambda g, s: (g, 0, 0)),) * 2,
        ),
        out_shape=(struct((4, 256, D), f32),) * 2,
        cost_estimate=cost(1e7, 1e7),
        name="update_small",
    )(
        scalars,
        small_own[:4].reshape(2, 2, 256, D),
        small_other[:4].reshape(2, 2, 256, D),
        attention_weight,
        attention_moment,
    )
    table_sum = kept_of(small_own[4], small_other[4])[: 4 * TABLE_ROWS : TABLE_ROWS].astype(f32)
    modulation_moment_new = vector_rate * modulation_moment + table_sum.reshape(2, 2, D)
    table_own = lax.dynamic_slice_in_dim(modulation, hid * 2, 2, 1)
    node_total = row_count * device_count
    modulation_new = table_own - 0.2 / math.sqrt(node_total) * modulation_moment_new
    return (
        output,
        features_grad,
        attention_moment_new,
        attention_new,
        up_moment_new,
        up_new,
        down_moment_new,
        down_new,
        modulation_moment_new,
        modulation_new,
    )


def solution(mesh):
    placed = (
        P(("nodes", "hid"), None),
        P(("nodes", "hid")),
        P(("nodes", "hid"), None),
        P(("nodes", "hid")),
        P(("nodes", "hid"), None),
        P(),
        P(None, "hid"),
        P("hid", None),
        P(),
        P(None, "hid", None),
        P(None, "hid"),
        P("hid", None),
        P(None, "hid", None),
    )
    return jax.shard_map(
        on_device,
        mesh=mesh,
        in_specs=placed,
        out_specs=(
            P(("nodes", "hid"), None),
            P(("nodes", "hid"), None),
            P(None, "hid", None),
            P(None, "hid", None),
            P(None, "hid"),
            P(None, "hid"),
            P("hid", None),
            P("hid", None),
            P(None, "hid", None),
            P(None, "hid", None),
        ),
        check_vma=False,
    )
```

time: 981 us -> 293 us (0.30)
  waiting for transfers between devices: 426 us -> 77.4 us
  matrix products: 307 us -> 0 us
  Pallas kernels: 0 us -> 138 us
  blocking collectives: 86.4 us -> 0 us
  local copies, waits for them, and re-layouts: 84.4 us -> 17.3 us
  starting transfers between devices: 11.5 us -> 32.3 us
  other arithmetic: 42.2 us -> 25.3 us
  between operations: 16.3 us -> 1.53 us
    psum x5 -> x0, waiting for transfers between devices: 323 us -> none  [the longest x4 323 us: on_device(): lax.psum(part_attn.astype(jnp.bfloat16), 'hid').astype(jnp.float32)]
    dot_general x59 -> x0, matrix products: 307 us -> none  [the longest x1 43.8 us: backward_block(): jnp.einsum('bkw,bhw->bhk', chooser, full_grads, precision=highest)]
    pallas_call x0 -> x13, Pallas kernels: none -> 138 us  [the longest x4 25.9 us: on_device(): pl.pallas_call(functools.partial(backward_kernel, h), grid=(1,), out_shap...]
    psum x2 -> x0, blocking collectives: 81.1 us -> none  [the longest x1 76 us: on_device(): lax.psum((attn_half, table_half, up_half, down_half), 'nodes')]
    ppermute x4 -> x27, waiting for transfers between devices: 23.8 us -> 77.4 us  [the longest x23 62.1 us: swap(): return lax.ppermute(value, AXES, pairs)]
    all_gather x2 -> x0, waiting for transfers between devices: 47.6 us -> none  [the longest x1 27.3 us: on_device(): inputs_all = lax.all_gather(second_in, 'hid', axis=0, tiled=True)]
    transpose x2 -> x0, local copies, waits for them, and re-layouts: 33.4 us -> none  [the longest x1 16.9 us: backward_block(): jnp.einsum('bhd,whd->bhw', grad_heads, window_values, preferred_element_t...]
    reduce_scatter x3 -> x0, waiting for transfers between devices: 30.8 us -> none  [the longest x1 20.3 us: on_device(): lax.psum_scatter(jnp.dot(activation, down_bf, preferred_element_type=jnp....]
  transfers between devices with their start and end apart: 14 -> 27, of which waited for: 12 -> 17; matrix products, arithmetic and copies ran while one was open for 21% -> 11% of each run, Pallas kernels for 0% -> 45%
where the time goes in v1:
time: 293 us; the launch traced here: 292 us
  Pallas kernels  138 us (47%)
  waiting for transfers between devices  77.4 us (26%)
  starting transfers between devices  32.3 us (11%)
  other arithmetic  25.3 us (9%)
  local copies, waits for them, and re-layouts  17.3 us (6%)
    ppermute x23, waiting for transfers between devices, swap(): return lax.ppermute(value, AXES, pairs)  62.1 us
    pallas_call x4, Pallas kernels, on_device(): pl.pallas_call(functools.partial(backward_kernel, h), grid=(1,), out_shap...  25.9 us
    ppermute x23, starting transfers between devices, swap(): return lax.ppermute(value, AXES, pairs)  23.8 us
    pallas_call x1, Pallas kernels, on_device(): pl.pallas_call(mlp_rest_kernel, out_shape=(chunk_shape, chunk_shape, stru...  20.3 us
    pallas_call x1, Pallas kernels, on_device(): pl.pallas_call(forward_kernel, out_shape=(struct((row_count, D), bf16), s...  18.4 us
    ppermute x4, waiting for transfers between devices, along(): return lax.ppermute(value, AXES, pairs)  15.3 us
    pallas_call x1, Pallas kernels, on_device(): pl.pallas_call(large_kernel, out_shape=(struct((2, D, CHUNK), bf16), stru...  14.5 us
    pallas_call x1, Pallas kernels, on_device(): pl.pallas_call(small_kernel, out_shape=struct((5, 256, D), bf16), in_spec...  12.7 us
  transfers between devices with their start and end apart: 27, of which 17 were waited for; matrix products, arithmetic and copies ran while one was open for 11% of the time, Pallas kernels for 45%

profile of v1, /device:TPU:0, one launch (start us, length us, event | category | flops | bytes accessed | tf_op | source)
XLA Modules:
  0.0 291.6 jit_solution(2265373210794889982)
XLA Ops:
  0.7 1.7 fusion.6
  2.5 3.0 %collective-permute-start.2 = (bf16[2,512,512]{2,1,0:T(8,128)(2,1)S(1)}, bf16[2,512,512]{2,1,0:T(8,128)(2,1)}, u32[]{:S(2)}, u32[]{:S(2)}) collective-permute-start(bf16[2,512,512]{2,1,0:T(8,128)(2,1)S(1)} %pad_maximum_fusion.1), channel_id=1, source_target_pairs={{0,1},{1,0},{2,3},{3,2},{4,5},{5,4},{6,7},{7,6},{8,9},{9,8},{10,11... | collective-permute-start | bytes 3145736 | tf_op jit(solution)/shard_map/ppermute | solution.py:603
  6.2 0.9 fusion.31
  7.2 2.0 collective-permute-start
  9.1 1.3 collective-permute-start.1
  10.5 3.8 %convert_element_type.96.weights.refs_19_ = bf16[4,512,512]{2,1,0:T(8,128)(2,1)} convert(f32[4,512,512]{2,1,0:T(8,128)} %weight.1) | non-fusion elementwise | flops 1048576 | bytes 6291456 | tf_op jit(solution)/shard_map/convert_element_type | solution.py:623
  15.5 9.1 %project.1 = (bf16[768,512]{1,0:T(8,128)(2,1)}, bf16[3,768,512]{2,1,0:T(8,128)(2,1)}, bf16[768,512]{1,0:T(8,128)(2,1)}) custom-call(bf16[768,512]{1,0:T(8,128)(2,1)} %refs_16_.1, f32[768,128]{1,0:T(8,128)} %get-tuple-element.103.pack.refs_17_, f32[8,512]{1,0:T(8,128)} %reshape.54.mod.refs_18_, bf16[4,512,512]{2,1,0:T(8,128)(2,1)} %convert_element_type.96.weights.refs_19_), custom_call_target="tpu_custom_call" | custom-call | flops 4000000000 | bytes 4000000 | tf_op jit(solution)/shard_map/project/pallas_call | solution.py:625
  24.6 7.1 %collective-permute-done.2.near = bf16[2,512,512]{2,1,0:T(8,128)(2,1)} collective-permute-done((bf16[2,512,512]{2,1,0:T(8,128)(2,1)S(1)}, bf16[2,512,512]{2,1,0:T(8,128)(2,1)}, u32[]{:S(2)}, u32[]{:S(2)}) %collective-permute-start.2) | collective-permute-done | bytes 1048608 | tf_op jit(solution)/shard_map/ppermute | solution.py:603
  31.7 5.3 %collective-permute-done.rim_low = bf16[192,640]{1,0:T(8,128)(2,1)S(1)} collective-permute-done((bf16[192,640]{1,0:T(8,128)(2,1)S(1)}, bf16[192,640]{1,0:T(8,128)(2,1)S(1)}, u32[]{:S(2)}, u32[]{:S(2)}) %collective-permute-start) | collective-permute-done | bytes 245792 | tf_op jit(solution)/shard_map/ppermute | solution.py:598
  37.0 2.2 collective-permute-done.1.rim_high
  40.0 18.4 %attend.1 = (bf16[768,512]{1,0:T(8,128)(2,1)}, f32[768,512]{1,0:T(8,128)}, bf16[768,512]{1,0:T(8,128)(2,1)}, bf16[2,1152,512]{2,1,0:T(8,128)(2,1)}, bf16[384,512...) custom-call(bf16[192,640]{1,0:T(8,128)(2,1)} %copy-done.19, bf16[192,640]{1,0:T(8,128)(2,1)} %copy-done.20, ...), custom_call_target="tpu_custom_call" | custom-call | flops 6000000000 | bytes 8000000 | tf_op jit(solution)/shard_map/attend/pallas_call | solution.py:638
  58.4 12.3 %mlp_own.1 = (f32[768,512]{1,0:T(8,128)}, f32[768,512]{1,0:T(8,128)}, bf16[2,2,2,128,512]{4,3,2,1,0:T(8,128)(2,1)}, bf16[2,2,2,128,512]{4,3,2,1,0:T(8,128)(2,1)}) custom-call(s32[5]{0:T(128)} %stack.110.scalars.refs_0_, bf16[768,512]{1,0:T(8,128)(2,1)} %get-tuple-element.57.second_in, bf16[768,512]{1,0:T(8,128)(2,1)} %cotangent.3, f32[512,1024]{1,0:T(8,128)} %up_weight.1, ...), custom_call_target="tpu_custom_call" | custom-call | flops 5000000000 | bytes 8000000 | tf_op jit(solution)/shard_map/mlp_own/pallas_call | solution.py:660
  70.6 1.3 broadcast_select_fusion.1
  72.1 20.3 %mlp_rest.1 = (bf16[2,2,2,128,512]{4,3,2,1,0:T(8,128)(2,1)}, bf16[2,2,2,128,512]{4,3,2,1,0:T(8,128)(2,1)}, bf16[768,512]{1,0:T(8,128)(2,1)}, f32[768,512]{1,0:T(...) custom-call(s32[5]{0:T(128)} %stack.110.scalars.refs_0_, ...), custom_call_target="tpu_custom_call" | custom-call | flops 6000000000 | bytes 12000000 | tf_op jit(solution)/shard_map/mlp_rest/pallas_call | solution.py:694
  92.4 2.5 broadcast_select_fusion
  95.3 3.9 %collective-permute-start.4 = (bf16[192,640]{1,0:T(8,128)(2,1)S(1)}, bf16[192,640]{1,0:T(8,128)(2,1)S(1)}, u32[]{:S(2)}, u32[]{:S(2)}) collective-permute-start(bf16[192,640]{1,0:T(8,128)(2,1)S(1)} %copy-done.22), channel_id=1, source_target_pairs={{0,1},{1,2},{2,3},{3,4},{4,5},{5,6},{6,7},{7,8},{8,9},{9,10},{10,1... | collective-permute-start | bytes 737288 | tf_op jit(solution)/shard_map/ppermute | solution.py:598
  99.3 1.3 collective-permute-start.5
  100.6 1.6 convert_add_fusion.2
  102.4 1.0 slice.158
  103.4 4.7 %collective-permute-done.4.grad_low.info_low = bf16[192,640]{1,0:T(8,128)(2,1)S(1)} collective-permute-done((bf16[192,640]{1,0:T(8,128)(2,1)S(1)}, bf16[192,640]{1,0:T(8,128)(2,1)S(1)}, u32[]{:S(2)}, u32[]{:S(2)}) %collective-permute-start.4) | collective-permute-done | bytes 245792 | tf_op jit(solution)/shard_map/ppermute | solution.py:598
  108.1 3.0 %collective-permute-done.5.grad_high.info_high = bf16[192,640]{1,0:T(8,128)(2,1)S(1)} collective-permute-done((bf16[192,640]{1,0:T(8,128)(2,1)S(1)}, bf16[192,640]{1,0:T(8,128)(2,1)S(1)}, u32[]{:S(2)}, u32[]{:S(2)}) %collective-permute-start.5) | collective-permute-done | bytes 245792 | tf_op jit(solution)/shard_map/ppermute | solution.py:598
  111.8 6.6 %attend_back.7 = (bf16[768,128]{1,0:T(8,128)(2,1)}, bf16[768,128]{1,0:T(8,128)(2,1)}, bf16[768,128]{1,0:T(8,128)(2,1)}) custom-call(bf16[3,768,512]{2,1,0:T(8,128)(2,1)} %get-tuple-element.55.qkv.query, bf16[2,1152,512]{2,1,0:T(8,128)(2,1)} %get-tuple-element.64.padded, bf16[768,512]{1,0:T(8,128)(2,1)} %get-tuple-element.65.grad, ...), custom_call_target="tpu_custom_call" | custom-call | flops 1000000000 | bytes 3000000 | tf_op jit(solution)/shard_map/attend_back/pallas_call | solution.py:814
  118.4 6.4 %attend_back.6 = (bf16[768,128]{1,0:T(8,128)(2,1)}, bf16[768,128]{1,0:T(8,128)(2,1)}, bf16[768,128]{1,0:T(8,128)(2,1)}) custom-call(bf16[3,768,512]{2,1,0:T(8,128)(2,1)} %get-tuple-element.55.qkv.query, bf16[2,1152,512]{2,1,0:T(8,128)(2,1)} %get-tuple-element.64.padded, bf16[768,512]{1,0:T(8,128)(2,1)} %get-tuple-element.65.grad, ...), custom_call_target="tpu_custom_call" | custom-call | flops 1000000000 | bytes 3000000 | tf_op jit(solution)/shard_map/attend_back/pallas_call | solution.py:814
  124.8 6.4 %attend_back.5 = (bf16[768,128]{1,0:T(8,128)(2,1)}, bf16[768,128]{1,0:T(8,128)(2,1)}, bf16[768,128]{1,0:T(8,128)(2,1)}) custom-call(bf16[3,768,512]{2,1,0:T(8,128)(2,1)} %get-tuple-element.55.qkv.query, bf16[2,1152,512]{2,1,0:T(8,128)(2,1)} %get-tuple-element.64.padded, bf16[768,512]{1,0:T(8,128)(2,1)} %get-tuple-element.65.grad, ...), custom_call_target="tpu_custom_call" | custom-call | flops 1000000000 | bytes 3000000 | tf_op jit(solution)/shard_map/attend_back/pallas_call | solution.py:814
  131.3 6.4 %attend_back.4 = (bf16[768,128]{1,0:T(8,128)(2,1)}, bf16[768,128]{1,0:T(8,128)(2,1)}, bf16[768,128]{1,0:T(8,128)(2,1)}) custom-call(bf16[3,768,512]{2,1,0:T(8,128)(2,1)} %get-tuple-element.55.qkv.query, bf16[2,1152,512]{2,1,0:T(8,128)(2,1)} %get-tuple-element.64.padded, bf16[768,512]{1,0:T(8,128)(2,1)} %get-tuple-element.65.grad, ...), custom_call_target="tpu_custom_call" | custom-call | flops 1000000000 | bytes 3000000 | tf_op jit(solution)/shard_map/attend_back/pallas_call | solution.py:814
  137.7 2.0 convert_add_fusion.1
  139.9 1.3 copy-done.9
  141.1 1.1 fusion.1
  142.3 10.5 %attend_weights.1 = (f32[768,512]{1,0:T(8,128)}, bf16[2,2,2,2,2,80,512]{6,5,4,3,2,1,0:T(8,128)(2,1)}) custom-call(s32[5]{0:T(128)} %stack.110.scalars.refs_0_, bf16[768,128]{1,0:T(8,128)(2,1)} %get-tuple-element.71.refs_1_, bf16[768,128]{1,0:T(8,128)(2,1)} %get-tuple-element.72.refs_2_, bf16[768,128]{1,0:T(8,128)(2,1)} %get-tuple-element.73.refs_3_, ...), custom_call_target="tpu_custom_call" | custom-call | flops 4000000000 | bytes 9000000 | tf_op jit(solution)/shard_map/attend_weights/pallas_call | solution.py:850
  152.7 1.4 slice_bitcast_fusion.1
  154.1 1.4 collective-permute-start.6
  155.6 1.8 collective-permute-done.18
  157.7 1.9 fusion
  159.6 1.0 fusion.8
  160.6 1.4 collective-permute-start.19
  164.0 1.0 dynamic_slice.22
  165.1 5.0 %collective-permute-done.19 = bf16[2,2,128,512]{3,2,1,0:T(8,128)(2,1)} collective-permute-done((bf16[2,2,128,512]{3,2,1,0:T(8,128)(2,1)}, bf16[2,2,128,512]{3,2,1,0:T(8,128)(2,1)}, u32[]{:S(2)}, u32[]{:S(2)}) %collective-permute-start.19) | collective-permute-done | bytes 524320 | tf_op jit(solution)/shard_map/ppermute | solution.py:603
  170.1 1.5 fusion.3
  171.6 1.9 collective-permute-start.20
  173.5 6.4 %collective-permute-done.7 = bf16[2,2,2,80,512]{4,3,2,1,0:T(8,128)(2,1)} collective-permute-done((bf16[2,2,2,80,512]{4,3,2,1,0:T(8,128)(2,1)}, bf16[2,2,2,80,512]{4,3,2,1,0:T(8,128)(2,1)}, u32[]{:S(2)}, u32[]{:S(2)}) %collective-permute-start.7) | collective-permute-done | bytes 655392 | tf_op jit(solution)/shard_map/ppermute | solution.py:603
  179.9 1.3 fusion.2
  182.1 3.2 %collective-permute-start.21 = (bf16[128,512]{1,0:T(8,128)(2,1)S(1)}, bf16[128,512]{1,0:T(8,128)(2,1)S(1)}, u32[]{:S(2)}, u32[]{:S(2)}) collective-permute-start(bf16[128,512]{1,0:T(8,128)(2,1)S(1)} %fusion.22), channel_id=1, source_target_pairs={{0,16},{1,17},{2,18},{3,19},{4,20},{5,21},{6,22},{7,23},{8,24},{9,... | collective-permute-start | bytes 393224 | tf_op jit(solution)/shard_map/ppermute | solution.py:603
  185.4 3.0 %collective-permute-done.8 = bf16[2,2,80,512]{3,2,1,0:T(8,128)(2,1)S(1)} collective-permute-done((bf16[2,2,80,512]{3,2,1,0:T(8,128)(2,1)S(1)}, bf16[2,2,80,512]{3,2,1,0:T(8,128)(2,1)S(1)}, u32[]{:S(2)}, u32[]{:S(2)}) %collective-permute-start.8) | collective-permute-done | bytes 327712 | tf_op jit(solution)/shard_map/ppermute | solution.py:603
  188.5 2.4 collective-permute-done.21
  190.9 1.0 fusion.18
  192.5 2.8 collective-permute-start.9
  195.3 5.5 %collective-permute-done.22 = bf16[128,512]{1,0:T(8,128)(2,1)S(1)} collective-permute-done((bf16[128,512]{1,0:T(8,128)(2,1)S(1)}, bf16[128,512]{1,0:T(8,128)(2,1)S(1)}, u32[]{:S(2)}, u32[]{:S(2)}) %collective-permute-start.22) | collective-permute-done | bytes 131104 | tf_op jit(solution)/shard_map/ppermute | solution.py:603
  201.0 2.2 collective-permute-start.10
  203.2 4.9 %collective-permute-done.23 = bf16[2,128,512]{2,1,0:T(8,128)(2,1)S(1)} collective-permute-done((bf16[2,128,512]{2,1,0:T(8,128)(2,1)S(1)}, bf16[2,128,512]{2,1,0:T(8,128)(2,1)S(1)}, u32[]{:S(2)}, u32[]{:S(2)}) %collective-permute-start.23) | collective-permute-done | bytes 262176 | tf_op jit(solution)/shard_map/ppermute | solution.py:603
  209.6 7.8 %collective-permute-done.24 = bf16[2,2,128,512]{3,2,1,0:T(8,128)(2,1)S(1)} collective-permute-done((bf16[2,2,128,512]{3,2,1,0:T(8,128)(2,1)S(1)}, bf16[2,2,128,512]{3,2,1,0:T(8,128)(2,1)S(1)}, u32[]{:S(2)}, u32[]{:S(2)}) %collective-permute-start.24) | collective-permute-done | bytes 524320 | tf_op jit(solution)/shard_map/ppermute | solution.py:603
  218.6 6.2 %collective-permute-done.11 = bf16[80,512]{1,0:T(8,128)(2,1)S(1)} collective-permute-done((bf16[80,512]{1,0:T(8,128)(2,1)S(1)}, bf16[80,512]{1,0:T(8,128)(2,1)S(1)}, u32[]{:S(2)}, u32[]{:S(2)}) %collective-permute-start.11) | collective-permute-done | bytes 81952 | tf_op jit(solution)/shard_map/ppermute | solution.py:603
  224.8 5.3 %collective-permute-done.12 = bf16[2,80,512]{2,1,0:T(8,128)(2,1)S(1)} collective-permute-done((bf16[2,80,512]{2,1,0:T(8,128)(2,1)S(1)}, bf16[2,80,512]{2,1,0:T(8,128)(2,1)S(1)}, u32[]{:S(2)}, u32[]{:S(2)}) %collective-permute-start.12) | collective-permute-done | bytes 163872 | tf_op jit(solution)/shard_map/ppermute | solution.py:603
  230.2 1.7 collective-permute-start.13
  231.9 6.1 %collective-permute-done.13 = bf16[2,2,80,512]{3,2,1,0:T(8,128)(2,1)S(1)} collective-permute-done((bf16[2,2,80,512]{3,2,1,0:T(8,128)(2,1)S(1)}, bf16[2,2,80,512]{3,2,1,0:T(8,128)(2,1)S(1)}, u32[]{:S(2)}, u32[]{:S(2)}) %collective-permute-start.13) | collective-permute-done | bytes 327712 | tf_op jit(solution)/shard_map/ppermute | solution.py:603
  238.0 1.7 collective-permute-start.14
  239.7 14.5 %ortho_large.1 = (bf16[2,512,512]{2,1,0:T(8,128)(2,1)}, bf16[2,512,512]{2,1,0:T(8,128)(2,1)}) custom-call(s32[5]{0:T(128)} %stack.110.scalars.refs_0_, bf16[2,2,2,128,512]{4,3,2,1,0:T(8,128)(2,1)} %copy-done.10, bf16[2,2,2,128,512]{4,3,2,1,0:T(8,128)(2,1)} %collective-permute-done.25.got), custom_call_target="tpu_custom_call" | custom-call | flops 10000000000 | bytes 6000000 | tf_op jit(solution)/shard_map/ortho_large/pallas_call | solution.py:885
  254.2 1.7 pad_maximum_fusion.own
  256.1 1.0 copy-done.18
  257.0 12.7 %ortho_small.1 = bf16[5,256,512]{2,1,0:T(8,128)(2,1)} custom-call(s32[5]{0:T(128)} %stack.110.scalars.refs_0_, bf16[2,2,2,80,512]{4,3,2,1,0:T(8,128)(2,1)} %copy-done.12, bf16[2,2,2,80,512]{4,3,2,1,0:T(8,128)(2,1)} %copy-done.18), custom_call_target="tpu_custom_call" | custom-call | flops 6000000000 | bytes 4000000 | tf_op jit(solution)/shard_map/ortho_small/pallas_call | solution.py:919
  270.0 2.3 slice.150
  272.9 1.7 fusion.14
  275.6 1.0 slice.151
  276.6 6.7 %update_small.1 = (f32[4,256,512]{2,1,0:T(8,128)}, f32[4,256,512]{2,1,0:T(8,128)}) custom-call(s32[5]{0:T(128)} %stack.110.scalars.refs_0_, bf16[2,2,256,512]{3,2,1,0:T(8,128)(2,1)} %bitcast.93, bf16[2,2,256,512]{3,2,1,0:T(8,128)(2,1)} %bitcast.94, f32[4,512,512]{2,1,0:T(8,128)} %weight.1, f32[4,256,512]{2,1,0:T(8,128)} %moment.1), custom_call_target="tpu_custom_call" | custom-call | flops 10000000 | bytes 10000000 | tf_op jit(solution)/shard_map/update_small/pallas_call | solution.py:936
  284.0 7.4 %update_large.1 = (f32[512,1024]{1,0:T(8,128)}, f32[512,1024]{1,0:T(8,128)}, f32[1024,512]{1,0:T(8,128)}, f32[1024,512]{1,0:T(8,128)}) custom-call(s32[5]{0:T(128)} %stack.110.scalars.refs_0_, bf16[2,2,512,512]{3,2,1,0:T(8,128)(2,1)} %copy-done.4, bf16[2,2,512,512]{3,2,1,0:T(8,128)(2,1)} %collective-permute-done.26.got, f32[512,1024]{1,0:T(8,128)} %up_weight.1, ...), custom_call_target="tpu_custom_call" | custom-call | flops 10000000 | bytes 20000000 | tf_op jit(solution)/shard_map/update_large/pallas_call | solution.py:896
  (115 shorter events, 13.7 us)
Async XLA Ops:
  0.7 4.9 %copy-start.13 = (s32[768,16]{0,1:T(8,128)S(1)}, s32[768,16]{0,1:T(8,128)}, u32[]{:S(2)}) copy-start(s32[768,16]{0,1:T(8,128)} %param.15) | copy-start | bytes 147460
  0.7 5.1 %copy-start.16 = (s32[768]{0:T(1024)S(1)}, s32[768]{0:T(1024)}, u32[]{:S(2)}) copy-start(s32[768]{0:T(1024)} %param.14) | copy-start | bytes 9220
  0.7 5.3 %copy-start.17 = (s32[768]{0:T(1024)S(1)}, s32[768]{0:T(1024)}, u32[]{:S(2)}) copy-start(s32[768]{0:T(1024)} %param.16) | copy-start | bytes 9220
  2.4 4.7 %copy-start.11 = (bf16[768,512]{1,0:T(8,128)(2,1)S(1)}, bf16[768,512]{1,0:T(8,128)(2,1)}, u32[]{:S(2)}) copy-start(bf16[768,512]{1,0:T(8,128)(2,1)} %refs_16_.1) | copy-start | bytes 2359300
  2.5 29.2 %collective-permute-start.2 = (bf16[2,512,512]{2,1,0:T(8,128)(2,1)S(1)}, bf16[2,512,512]{2,1,0:T(8,128)(2,1)}, u32[]{:S(2)}, u32[]{:S(2)}) collective-permute-start(bf16[2,512,512]{2,1,0:T(8,128)(2,1)S(1)} %pad_maximum_fusion.1), channel_id=1, source_target_pairs={{0,1},{1,0},{2,3},{3,2},{4,5},{5,4},{6,7},{7,6},{8,9},{9,8},{10,11... | collective-permute-start | bytes 3145736 | tf_op jit(solution)/shard_map/ppermute | solution.py:603
  7.2 29.8 %collective-permute-start = (bf16[192,640]{1,0:T(8,128)(2,1)S(1)}, bf16[192,640]{1,0:T(8,128)(2,1)S(1)}, u32[]{:S(2)}, u32[]{:S(2)}) collective-permute-start(bf16[192,640]{1,0:T(8,128)(2,1)S(1)} %get-tuple-element.105), channel_id=1, source_target_pairs={{0,1},{1,2},{2,3},{3,4},{4,5},{5,6},{6,7},{7,8},{8,9},{9,10},{10,1... | collective-permute-start | bytes 737288 | tf_op jit(solution)/shard_map/ppermute | solution.py:598
  9.1 30.1 %collective-permute-start.1 = (bf16[192,640]{1,0:T(8,128)(2,1)S(1)}, bf16[192,640]{1,0:T(8,128)(2,1)S(1)}, u32[]{:S(2)}, u32[]{:S(2)}) collective-permute-start(bf16[192,640]{1,0:T(8,128)(2,1)S(1)} %get-tuple-element.104), channel_id=1, source_target_pairs={{1,0},{2,1},{3,2},{4,3},{5,4},{6,5},{7,6},{8,7},{9,8},{10,9},{11,1... | collective-permute-start | bytes 737288 | tf_op jit(solution)/shard_map/ppermute | solution.py:598
  10.5 3.8 %copy-start.14 = (f32[2,4,512]{2,1,0:T(4,128)S(1)}, f32[2,4,512]{2,1,0:T(4,128)}, u32[]{:S(2)}) copy-start(f32[2,4,512]{2,1,0:T(4,128)} %param.21) | copy-start | bytes 49156
  31.7 40.3 %collective-permute-start.3 = (bf16[2,512,512]{2,1,0:T(8,128)(2,1)}, bf16[2,512,512]{2,1,0:T(8,128)(2,1)}, u32[]{:S(2)}, u32[]{:S(2)}) collective-permute-start(bf16[2,512,512]{2,1,0:T(8,128)(2,1)} %collective-permute-done.2.near), channel_id=1, source_target_pairs={{0,2},{1,3},{2,0},{3,1},{4,6},{5,7},{6,4},{7,5},{8,10},{9,11},{10,... | collective-permute-start | bytes 3145736 | tf_op jit(solution)/shard_map/ppermute | solution.py:603
  37.0 2.2 copy-start.19
  39.3 0.7 copy-start.20
  72.0 28.6 %collective-permute-start.16 = (bf16[2,2,2,128,512]{4,3,2,1,0:T(8,128)(2,1)S(1)}, bf16[2,2,2,128,512]{4,3,2,1,0:T(8,128)(2,1)}, u32[]{:S(2)}, u32[]{:S(2)}) collective-permute-start(bf16[2,2,2,128,512]{4,3,2,1,0:T(8,128)(2,1)S(1)} %broadcast_select_fusion.1), channel_id=1, source_target_pairs={{0,2},{1,3},{2,0},{3,1},{4,6},{5,7},{6,4},{7,5},{8,10},{9,11},{10,... | collective-permute-start | bytes 3145736 | tf_op jit(solution)/shard_map/ppermute | solution.py:603
  92.3 3.0 %copy-start.22 = (bf16[192,640]{1,0:T(8,128)(2,1)S(1)}, bf16[192,640]{1,0:T(8,128)(2,1)}, u32[]{:S(2)}) copy-start(bf16[192,640]{1,0:T(8,128)(2,1)} %get-tuple-element.69) | copy-start | bytes 737284
  92.3 6.9 %copy-start.21 = (bf16[192,640]{1,0:T(8,128)(2,1)S(1)}, bf16[192,640]{1,0:T(8,128)(2,1)}, u32[]{:S(2)}) copy-start(bf16[192,640]{1,0:T(8,128)(2,1)} %get-tuple-element.70) | copy-start | bytes 737284
  92.4 8.3 %copy-start.6 = (bf16[2,2,2,128,512]{4,3,2,1,0:T(8,128)(2,1)S(1)}, bf16[2,2,2,128,512]{4,3,2,1,0:T(8,128)(2,1)}, u32[]{:S(2)}) copy-start(bf16[2,2,2,128,512]{4,3,2,1,0:T(8,128)(2,1)} %get-tuple-element.90) | copy-start | bytes 3145732
  92.4 8.3 %copy-start.7 = (bf16[2,2,2,128,512]{4,3,2,1,0:T(8,128)(2,1)S(1)}, bf16[2,2,2,128,512]{4,3,2,1,0:T(8,128)(2,1)}, u32[]{:S(2)}) copy-start(bf16[2,2,2,128,512]{4,3,2,1,0:T(8,128)(2,1)} %get-tuple-element.91) | copy-start | bytes 3145732
  94.8 42.9 %collective-permute-start.17 = (bf16[2,2,2,128,512]{4,3,2,1,0:T(8,128)(2,1)}, bf16[2,2,2,128,512]{4,3,2,1,0:T(8,128)(2,1)}, u32[]{:S(2)}, u32[]{:S(2)}) collective-permute-start(bf16[2,2,2,128,512]{4,3,2,1,0:T(8,128)(2,1)} %broadcast_select_fusion), channel_id=1, source_target_pairs={{0,2},{1,3},{2,0},{3,1},{4,6},{5,7},{6,4},{7,5},{8,10},{9,11},{10,... | collective-permute-start | bytes 3145736 | tf_op jit(solution)/shard_map/ppermute | solution.py:603
  95.3 12.8 %collective-permute-start.4 = (bf16[192,640]{1,0:T(8,128)(2,1)S(1)}, bf16[192,640]{1,0:T(8,128)(2,1)S(1)}, u32[]{:S(2)}, u32[]{:S(2)}) collective-permute-start(bf16[192,640]{1,0:T(8,128)(2,1)S(1)} %copy-done.22), channel_id=1, source_target_pairs={{0,1},{1,2},{2,3},{3,4},{4,5},{5,6},{6,7},{7,8},{8,9},{9,10},{10,1... | collective-permute-start | bytes 737288 | tf_op jit(solution)/shard_map/ppermute | solution.py:598
  99.3 11.8 %collective-permute-start.5 = (bf16[192,640]{1,0:T(8,128)(2,1)S(1)}, bf16[192,640]{1,0:T(8,128)(2,1)S(1)}, u32[]{:S(2)}, u32[]{:S(2)}) collective-permute-start(bf16[192,640]{1,0:T(8,128)(2,1)S(1)} %copy-done.21), channel_id=1, source_target_pairs={{1,0},{2,1},{3,2},{4,3},{5,4},{6,5},{7,6},{8,7},{9,8},{10,9},{11,1... | collective-permute-start | bytes 737288 | tf_op jit(solution)/shard_map/ppermute | solution.py:598
  102.3 53.3 %copy-start.2 = (f32[2,2,2,128,512]{4,3,2,1,0:T(8,128)}, f32[2,2,2,128,512]{4,3,2,1,0:T(8,128)S(1)}, u32[]{:S(2)}) copy-start(f32[2,2,2,128,512]{4,3,2,1,0:T(8,128)S(1)} %convert_add_fusion.2) | copy-start | bytes 6291460
  108.1 3.0 %copy-start = (bf16[192,640]{1,0:T(8,128)(2,1)}, bf16[192,640]{1,0:T(8,128)(2,1)S(1)}, u32[]{:S(2)}) copy-start(bf16[192,640]{1,0:T(8,128)(2,1)S(1)} %collective-permute-done.4.grad_low.info_low) | copy-start | bytes 737284
  111.1 0.7 copy-start.1
  139.7 2.6 copy-start.3
  139.7 1.4 copy-start.9
  142.3 15.1 %collective-permute-start.18 = (bf16[2,2,2,128,512]{4,3,2,1,0:T(8,128)(2,1)}, bf16[2,2,2,128,512]{4,3,2,1,0:T(8,128)(2,1)}, u32[]{:S(2)}, u32[]{:S(2)}) collective-permute-start(bf16[2,2,2,128,512]{4,3,2,1,0:T(8,128)(2,1)} %fusion.1), channel_id=1, source_target_pairs={{0,4},{1,5},{2,10},{3,11},{4,0},{5,1},{6,14},{7,15},{8,12},{9,13},... | collective-permute-start | bytes 3145736 | tf_op jit(solution)/shard_map/ppermute | solution.py:603
  154.1 7.9 %collective-permute-start.6 = (bf16[2,2,2,2,80,512]{5,4,3,2,1,0:T(8,128)(2,1)S(1)}, bf16[2,2,2,2,80,512]{5,4,3,2,1,0:T(8,128)(2,1)S(1)}, u32[]{:S(2)}, u32[]{:S(2)}) collective-permute-start(bf16[2,2,2,2,80,512]{5,4,3,2,1,0:T(8,128)(2,1)S(1)} %slice_bitcast_fusion.1), channel_id=1, source_target_pairs={{0,2},{1,3},{2,0},{3,1},{4,6},{5,7},{6,4},{7,5},{8,10},{9,11},{10,... | collective-permute-start | bytes 3932168 | tf_op jit(solution)/shard_map/ppermute | solution.py:603
  155.6 1.8 slice-start
  155.6 1.8 slice-start.1
  155.6 1.9 slice-start.2
  155.6 2.2 slice-start.3
  155.6 6.4 %copy-start.8 = (bf16[2,2,2,2,2,80,512]{6,5,4,3,2,1,0:T(8,128)(2,1)S(1)}, bf16[2,2,2,2,2,80,512]{6,5,4,3,2,1,0:T(8,128)(2,1)}, u32[]{:S(2)}) copy-start(bf16[2,2,2,2,2,80,512]{6,5,4,3,2,1,0:T(8,128)(2,1)} %get-tuple-element.87) | copy-start | bytes 7864324
  159.6 2.9 copy-start.5
  160.6 9.5 %collective-permute-start.19 = (bf16[2,2,128,512]{3,2,1,0:T(8,128)(2,1)}, bf16[2,2,128,512]{3,2,1,0:T(8,128)(2,1)}, u32[]{:S(2)}, u32[]{:S(2)}) collective-permute-start(bf16[2,2,128,512]{3,2,1,0:T(8,128)(2,1)} %fusion.8), channel_id=1, source_target_pairs={{0,1},{1,0},{2,6},{3,7},{4,5},{5,4},{6,2},{7,3},{8,9},{9,8},{10,14... | collective-permute-start | bytes 1572872 | tf_op jit(solution)/shard_map/ppermute | solution.py:603
  163.4 16.5 %collective-permute-start.7 = (bf16[2,2,2,80,512]{4,3,2,1,0:T(8,128)(2,1)}, bf16[2,2,2,80,512]{4,3,2,1,0:T(8,128)(2,1)}, u32[]{:S(2)}, u32[]{:S(2)}) collective-permute-start(bf16[2,2,2,80,512]{4,3,2,1,0:T(8,128)(2,1)} %fusion.4), channel_id=1, source_target_pairs={{0,1},{1,0},{2,6},{3,7},{4,5},{5,4},{6,2},{7,3},{8,9},{9,8},{10,14... | collective-permute-start | bytes 1966088 | tf_op jit(solution)/shard_map/ppermute | solution.py:603
  171.6 10.4 %collective-permute-start.20 = (bf16[2,128,512]{2,1,0:T(8,128)(2,1)S(1)}, bf16[2,128,512]{2,1,0:T(8,128)(2,1)S(1)}, u32[]{:S(2)}, u32[]{:S(2)}) collective-permute-start(bf16[2,128,512]{2,1,0:T(8,128)(2,1)S(1)} %fusion.13), channel_id=1, source_target_pairs={{0,8},{1,9},{2,3},{3,2},{4,12},{5,13},{6,7},{7,6},{8,0},{9,1},{10,... | collective-permute-start | bytes 786440 | tf_op jit(solution)/shard_map/ppermute | solution.py:603
  181.2 7.1 %collective-permute-start.8 = (bf16[2,2,80,512]{3,2,1,0:T(8,128)(2,1)S(1)}, bf16[2,2,80,512]{3,2,1,0:T(8,128)(2,1)S(1)}, u32[]{:S(2)}, u32[]{:S(2)}) collective-permute-start(bf16[2,2,80,512]{3,2,1,0:T(8,128)(2,1)S(1)} %fusion.11), channel_id=1, source_target_pairs={{0,4},{1,5},{2,10},{3,11},{4,0},{5,1},{6,14},{7,15},{8,12},{9,13},... | collective-permute-start | bytes 983048 | tf_op jit(solution)/shard_map/ppermute | solution.py:603
  182.1 8.8 %collective-permute-start.21 = (bf16[128,512]{1,0:T(8,128)(2,1)S(1)}, bf16[128,512]{1,0:T(8,128)(2,1)S(1)}, u32[]{:S(2)}, u32[]{:S(2)}) collective-permute-start(bf16[128,512]{1,0:T(8,128)(2,1)S(1)} %fusion.22), channel_id=1, source_target_pairs={{0,16},{1,17},{2,18},{3,19},{4,20},{5,21},{6,22},{7,23},{8,24},{9,... | collective-permute-start | bytes 393224 | tf_op jit(solution)/shard_map/ppermute | solution.py:603
  191.9 8.8 %collective-permute-start.22 = (bf16[128,512]{1,0:T(8,128)(2,1)S(1)}, bf16[128,512]{1,0:T(8,128)(2,1)S(1)}, u32[]{:S(2)}, u32[]{:S(2)}) collective-permute-start(bf16[128,512]{1,0:T(8,128)(2,1)S(1)} %fusion.18), channel_id=1, source_target_pairs={{0,16},{1,17},{2,18},{3,19},{4,20},{5,21},{6,22},{7,23},{8,24},{9,... | collective-permute-start | bytes 393224 | tf_op jit(solution)/shard_map/ppermute | solution.py:603
  192.5 8.4 %collective-permute-start.9 = (bf16[2,80,512]{2,1,0:T(8,128)(2,1)S(1)}, bf16[2,80,512]{2,1,0:T(8,128)(2,1)S(1)}, u32[]{:S(2)}, u32[]{:S(2)}) collective-permute-start(bf16[2,80,512]{2,1,0:T(8,128)(2,1)S(1)} %fusion.20), channel_id=1, source_target_pairs={{0,8},{1,9},{2,3},{3,2},{4,12},{5,13},{6,7},{7,6},{8,0},{9,1},{10,... | collective-permute-start | bytes 491528 | tf_op jit(solution)/shard_map/ppermute | solution.py:603
  200.8 7.3 %collective-permute-start.23 = (bf16[2,128,512]{2,1,0:T(8,128)(2,1)S(1)}, bf16[2,128,512]{2,1,0:T(8,128)(2,1)S(1)}, u32[]{:S(2)}, u32[]{:S(2)}) collective-permute-start(bf16[2,128,512]{2,1,0:T(8,128)(2,1)S(1)} %get-tuple-element.111), channel_id=1, source_target_pairs={{0,8},{1,9},{2,3},{3,2},{4,12},{5,13},{6,7},{7,6},{8,0},{9,1},{10,... | collective-permute-start | bytes 786440 | tf_op jit(solution)/shard_map/ppermute | solution.py:603
  201.0 7.7 %collective-permute-start.10 = (bf16[80,512]{1,0:T(8,128)(2,1)S(1)}, bf16[80,512]{1,0:T(8,128)(2,1)S(1)}, u32[]{:S(2)}, u32[]{:S(2)}) collective-permute-start(bf16[80,512]{1,0:T(8,128)(2,1)S(1)} %fusion.25), channel_id=1, source_target_pairs={{0,16},{1,17},{2,18},{3,19},{4,20},{5,21},{6,22},{7,23},{8,24},{9,... | collective-permute-start | bytes 245768 | tf_op jit(solution)/shard_map/ppermute | solution.py:603
  208.2 9.2 %collective-permute-start.24 = (bf16[2,2,128,512]{3,2,1,0:T(8,128)(2,1)S(1)}, bf16[2,2,128,512]{3,2,1,0:T(8,128)(2,1)S(1)}, u32[]{:S(2)}, u32[]{:S(2)}) collective-permute-start(bf16[2,2,128,512]{3,2,1,0:T(8,128)(2,1)S(1)} %get-tuple-element.107), channel_id=1, source_target_pairs={{0,1},{1,0},{2,6},{3,7},{4,5},{5,4},{6,2},{7,3},{8,9},{9,8},{10,14... | collective-permute-start | bytes 1572872 | tf_op jit(solution)/shard_map/ppermute | solution.py:603
  217.5 22.2 %copy-start.10 = (bf16[2,2,2,128,512]{4,3,2,1,0:T(8,128)(2,1)}, bf16[2,2,2,128,512]{4,3,2,1,0:T(8,128)(2,1)S(1)}, u32[]{:S(2)}) copy-start(bf16[2,2,2,128,512]{4,3,2,1,0:T(8,128)(2,1)S(1)} %pad_maximum_fusion.2.kept) | copy-start | bytes 3145732
  217.5 22.1 %collective-permute-start.25 = (bf16[2,2,2,128,512]{4,3,2,1,0:T(8,128)(2,1)S(1)}, bf16[2,2,2,128,512]{4,3,2,1,0:T(8,128)(2,1)}, u32[]{:S(2)}, u32[]{:S(2)}) collective-permute-start(bf16[2,2,2,128,512]{4,3,2,1,0:T(8,128)(2,1)S(1)} %pad_maximum_fusion.2.kept), channel_id=1, source_target_pairs={{0,4},{1,5},{2,10},{3,11},{4,0},{5,1},{6,14},{7,15},{8,12},{9,13},... | collective-permute-start | bytes 3145736 | tf_op jit(solution)/shard_map/ppermute | solution.py:603
  217.7 7.1 %collective-permute-start.11 = (bf16[80,512]{1,0:T(8,128)(2,1)S(1)}, bf16[80,512]{1,0:T(8,128)(2,1)S(1)}, u32[]{:S(2)}, u32[]{:S(2)}) collective-permute-start(bf16[80,512]{1,0:T(8,128)(2,1)S(1)} %get-tuple-element.115), channel_id=1, source_target_pairs={{0,16},{1,17},{2,18},{3,19},{4,20},{5,21},{6,22},{7,23},{8,24},{9,... | collective-permute-start | bytes 245768 | tf_op jit(solution)/shard_map/ppermute | solution.py:603
  224.7 5.4 %collective-permute-start.12 = (bf16[2,80,512]{2,1,0:T(8,128)(2,1)S(1)}, bf16[2,80,512]{2,1,0:T(8,128)(2,1)S(1)}, u32[]{:S(2)}, u32[]{:S(2)}) collective-permute-start(bf16[2,80,512]{2,1,0:T(8,128)(2,1)S(1)} %get-tuple-element.113), channel_id=1, source_target_pairs={{0,8},{1,9},{2,3},{3,2},{4,12},{5,13},{6,7},{7,6},{8,0},{9,1},{10,... | collective-permute-start | bytes 491528 | tf_op jit(solution)/shard_map/ppermute | solution.py:603
  230.2 7.7 %collective-permute-start.13 = (bf16[2,2,80,512]{3,2,1,0:T(8,128)(2,1)S(1)}, bf16[2,2,80,512]{3,2,1,0:T(8,128)(2,1)S(1)}, u32[]{:S(2)}, u32[]{:S(2)}) collective-permute-start(bf16[2,2,80,512]{3,2,1,0:T(8,128)(2,1)S(1)} %get-tuple-element.109), channel_id=1, source_target_pairs={{0,4},{1,5},{2,10},{3,11},{4,0},{5,1},{6,14},{7,15},{8,12},{9,13},... | collective-permute-start | bytes 983048 | tf_op jit(solution)/shard_map/ppermute | solution.py:603
  238.0 16.2 %copy-start.12 = (bf16[2,2,2,80,512]{4,3,2,1,0:T(8,128)(2,1)}, bf16[2,2,2,80,512]{4,3,2,1,0:T(8,128)(2,1)S(1)}, u32[]{:S(2)}) copy-start(bf16[2,2,2,80,512]{4,3,2,1,0:T(8,128)(2,1)S(1)} %pad_maximum_fusion.3.kept) | copy-start | bytes 1966084
  238.0 18.0 %collective-permute-start.14 = (bf16[2,2,2,80,512]{4,3,2,1,0:T(8,128)(2,1)S(1)}, bf16[2,2,2,80,512]{4,3,2,1,0:T(8,128)(2,1)S(1)}, u32[]{:S(2)}, u32[]{:S(2)}) collective-permute-start(bf16[2,2,2,80,512]{4,3,2,1,0:T(8,128)(2,1)S(1)} %pad_maximum_fusion.3.kept), channel_id=1, source_target_pairs={{0,1},{1,0},{2,6},{3,7},{4,5},{5,4},{6,2},{7,3},{8,9},{9,8},{10,14... | collective-permute-start | bytes 1966088 | tf_op jit(solution)/shard_map/ppermute | solution.py:603
  256.0 13.7 %copy-start.4 = (bf16[2,2,512,512]{3,2,1,0:T(8,128)(2,1)}, bf16[2,2,512,512]{3,2,1,0:T(8,128)(2,1)S(1)}, u32[]{:S(2)}) copy-start(bf16[2,2,512,512]{3,2,1,0:T(8,128)(2,1)S(1)} %pad_maximum_fusion.own) | copy-start | bytes 6291460
  256.0 28.0 %collective-permute-start.26 = (bf16[2,2,512,512]{3,2,1,0:T(8,128)(2,1)S(1)}, bf16[2,2,512,512]{3,2,1,0:T(8,128)(2,1)}, u32[]{:S(2)}, u32[]{:S(2)}) collective-permute-start(bf16[2,2,512,512]{3,2,1,0:T(8,128)(2,1)S(1)} %pad_maximum_fusion.own), channel_id=1, source_target_pairs={{0,2},{1,3},{2,0},{3,1},{4,6},{5,7},{6,4},{7,5},{8,10},{9,11},{10,... | collective-permute-start | bytes 6291464 | tf_op jit(solution)/shard_map/ppermute | solution.py:603
  256.1 1.0 copy-start.18
  269.7 3.2 %collective-permute-start.15 = (bf16[5,256,512]{2,1,0:T(8,128)(2,1)}, bf16[5,256,512]{2,1,0:T(8,128)(2,1)S(1)}, u32[]{:S(2)}, u32[]{:S(2)}) collective-permute-start(bf16[5,256,512]{2,1,0:T(8,128)(2,1)} %ortho_small.1), channel_id=1, source_target_pairs={{0,2},{1,3},{2,0},{3,1},{4,6},{5,7},{6,4},{7,5},{8,10},{9,11},{10,... | collective-permute-start | bytes 3932168 | tf_op jit(solution)/shard_map/ppermute | solution.py:603
  276.6 6.7 %copy-start.15 = (f32[2,2,512]{2,1,0:T(2,128)S(1)}, f32[2,2,512]{2,1,0:T(2,128)}, u32[]{:S(2)}) copy-start(f32[2,2,512]{2,1,0:T(2,128)} %param.25) | copy-start | bytes 24580
